TPU v7x, 512 devices: a whole 4x8x8 slice. The times are simulated.
512 devices in a mesh: row: 16 (over z_hi, x, core), col: 32 (over z_lo, y).
Axes of the slice: x: 4, y: 8, z: 8 (z_hi: 2, z_lo: 4; z = z_hi * 4 + z_lo), core: 2. Of those that a mesh axis runs over, the one named last changes fastest.
Arguments:
- object_slices: bfloat16 [2, 2, 4096, 8192], P(None, None, 'row', 'col'), may hold values from -4 to 4
- probe_wave_parts: float32 [32, 2, 256, 256], P('col'), may hold values from -4 to 4
- prop_phase: float32 [256, 256], replicated, may hold values from -3.140625 to 3.140625
- measured: float32 [2048, 256, 256], P(('row', 'col')), may hold values from 0 to 2
- positions: int32 [2048, 2], P(('row', 'col')), may hold values from 0 to 255
Outputs:
- grad_object: float32 [2, 2, 4096, 8192], P(None, None, 'row', 'col')
- probe_grad: float32 [32, 2, 256, 256], P('col')
Inputs may be any that keep to these rules, and one draw needn't show every extreme that they name: Each device holds only positions inside its own tile; a window covers the tile's rows from its centre row - 128 to centre row + 127, likewise columns.
All inputs are finite; a program needn't handle non-finite values.
Results may differ from a plain program's by a relative error of at most 0.015.
Values may be sent and summed in bfloat16 or wider, within the bound.
A program may use at most 64 MiB of HBM per device.

v0:
```python
import math

import jax
import jax.numpy as jnp
from jax import lax
from jax.sharding import PartitionSpec as P


def extended_2(x, sides, width):
    for axis, dim in sides:
        count, length = (lax.axis_size(axis), x.shape[dim])
        up = [(i, (i + 1) % count) for i in range(count - 1)]
        down = [(j, i) for i, j in up]
        last = lax.slice_in_dim(x, length - width, length, axis=dim)
        first = lax.slice_in_dim(x, 0, width, axis=dim)
        before = lax.ppermute(last, axis, up)
        after = lax.ppermute(first, axis, down)
        x = jnp.concatenate([before, x, after], axis=dim)
    return x


def dft_tables(length, direction):
    numbers = jnp.arange(length, dtype=jnp.int32)
    phase_int = numbers[:, None] * numbers[None, :] % length
    angles = 2.0 * math.pi / length * phase_int.astype(jnp.float32)
    cosine = jnp.cos(angles) / math.sqrt(length)
    sine_part = direction * jnp.sin(angles) / math.sqrt(length)
    matrix = jnp.stack([jnp.stack([cosine, sine_part]), jnp.stack([-sine_part, cosine])])
    return matrix.astype(jnp.bfloat16)


def transform(wave_in, matrix):
    rounded = wave_in.astype(jnp.bfloat16)
    halfway = jnp.einsum(
        "pqab,nqbc->npac", matrix, rounded, preferred_element_type=jnp.float32
    ).astype(jnp.bfloat16)
    return jnp.einsum("nqac,pqcd->npad", halfway, matrix, preferred_element_type=jnp.float32)


def complex_mul(former, latter):
    real_part = former[:, 0] * latter[:, 0] - former[:, 1] * latter[:, 1]
    imag_part = former[:, 0] * latter[:, 1] + former[:, 1] * latter[:, 0]
    return jnp.stack([real_part, imag_part], axis=1)


def conj_mul(former, latter):
    real_part = former[:, 0] * latter[:, 0] + former[:, 1] * latter[:, 1]
    imag_part = former[:, 0] * latter[:, 1] - former[:, 1] * latter[:, 0]
    return jnp.stack([real_part, imag_part], axis=1)


def gradient_per_window(
    extended,
    window_corners,
    probe_wave_parts,
    fresnel_propagator,
    measured,
    forward_transform,
    inverse_transform,
):
    zero_index = jnp.zeros((), jnp.int32)
    win_size = probe_wave_parts.shape[1]
    windows = jax.vmap(
        lambda start_pair: lax.dynamic_slice(
            extended,
            (zero_index, zero_index, start_pair[0], start_pair[1]),
            (2, 2, win_size, win_size),
        )
    )(window_corners)
    windows = windows.astype(jnp.float32)
    slice_one = windows[:, 0]
    slice_two = windows[:, 1]
    first_exit = complex_mul(probe_wave_parts[None], slice_one)
    spectrum = complex_mul(fresnel_propagator[None], transform(first_exit, forward_transform))
    wavefield = transform(spectrum, inverse_transform)
    detector = transform(complex_mul(wavefield, slice_two), forward_transform)
    intensity = detector[:, 0] * detector[:, 0] + detector[:, 1] * detector[:, 1]
    misfit = (intensity - measured)[:, None] * detector
    back_two = transform(misfit, inverse_transform)
    grad_second = conj_mul(wavefield, back_two)
    back_spec = transform(conj_mul(slice_two, back_two), forward_transform)
    back_one = transform(conj_mul(fresnel_propagator[None], back_spec), inverse_transform)
    grad_first = conj_mul(probe_wave_parts[None], back_one)
    probe_sum = jnp.sum(conj_mul(slice_one, back_one), axis=0)
    illumination = jnp.sum(
        slice_one[:, 0] * slice_one[:, 0] + slice_one[:, 1] * slice_one[:, 1], axis=0
    )
    return (jnp.stack([grad_first, grad_second], axis=1), probe_sum, illumination)


def add_windows(total, window_gradient_stack, window_corners):
    zero_index = jnp.zeros((), jnp.int32)
    win_size = window_gradient_stack.shape[-1]

    def place_one(number, current):
        start_pair = window_corners[number]
        where = (zero_index, zero_index, start_pair[0], start_pair[1])
        present = lax.dynamic_slice(current, where, (2, 2, win_size, win_size))
        return lax.dynamic_update_slice(current, present + window_gradient_stack[number], where)

    return lax.fori_loop(0, window_gradient_stack.shape[0], place_one, total)


def fold_cols(gradient):
    extent = gradient.shape[3]
    half_win = extent // 4
    tile_size = extent // 2
    rim_pairs = jnp.concatenate(
        (gradient[:, :, :, :half_win], gradient[:, :, :, tile_size + half_win :]), axis=3
    )
    received = extended_2(rim_pairs, (("col", 3),), half_win)
    folded = gradient[:, :, :, half_win : tile_size + half_win]
    folded = folded.at[:, :, :, :half_win].add(received[:, :, :, :half_win])
    folded = folded.at[:, :, :, tile_size - half_win :].add(
        received[:, :, :, tile_size + half_win :]
    )
    return folded


def fold_rows(gradient):
    extent = gradient.shape[2]
    half_win = extent // 4
    tile_size = extent // 2
    rim_pairs = jnp.concatenate(
        (gradient[:, :, :half_win], gradient[:, :, tile_size + half_win :]), axis=2
    )
    received = extended_2(rim_pairs, (("row", 2),), half_win)
    folded = gradient[:, :, half_win : tile_size + half_win]
    folded = folded.at[:, :, :half_win].add(received[:, :, :half_win])
    folded = folded.at[:, :, tile_size - half_win :].add(received[:, :, tile_size + half_win :])
    return folded


def on_device(object_slices, probe_wave_parts, prop_phase, measured, positions):
    probe_here = probe_wave_parts[0]
    win_size = probe_here.shape[1]
    half_win = win_size // 2
    extended = extended_2(object_slices, (("row", 2), ("col", 3)), half_win)
    forward_transform = dft_tables(win_size, 1.0)
    inverse_transform = dft_tables(win_size, -1.0)
    fresnel_propagator = jnp.stack([jnp.cos(prop_phase), jnp.sin(prop_phase)])
    window_gradient_stack, probe_sum, illumination = gradient_per_window(
        extended,
        positions,
        probe_here,
        fresnel_propagator,
        measured,
        forward_transform,
        inverse_transform,
    )
    grad_ext = add_windows(jnp.zeros(extended.shape, jnp.float32), window_gradient_stack, positions)
    grad_object = fold_rows(fold_cols(grad_ext))
    totals = lax.psum((probe_sum, illumination), "row")
    probe_grad = totals[0] / jnp.sqrt(totals[1] + 1e-06)[None]
    return (grad_object, probe_grad[None])


def solution(mesh):
    return jax.shard_map(
        on_device,
        mesh=mesh,
        in_specs=(
            P(None, None, "row", "col"),
            P("col", None, None, None),
            P(),
            P(("row", "col"), None, None),
            P(("row", "col"), None),
        ),
        out_specs=(P(None, None, "row", "col"), P("col", None, None, None)),
        check_vma=False,
    )
```

profile of v0, /device:TPU:1, one launch (start us, length us, event | category | flops | bytes accessed | tf_op | source)
XLA Modules:
  0.0 417.1 jit_solution(17855076346696729461)
XLA Ops:
  9.1 8.7 %collective-permute-start.1 = (bf16[2,2,128,256]{3,2,1,0:T(8,128)(2,1)}, bf16[2,2,128,256]{3,2,1,0:T(8,128)(2,1)}, u32[]{:S(2)}, u32[]{:S(2)}) collective-permute-start(bf16[2,2,128,256]{3,2,1,0:T(8,128)(2,1)} %get-tuple-element.203), channel_id=1, source_target_pairs={{32,0},{64,32},{96,64},{128,96},{160,128},{192,160},{224,192},{256... | collective-permute-start | bytes 786440 | tf_op jit(solution)/shard_map/ppermute | solution.py:17
  17.9 1.9 collective-permute-start
  36.2 7.7 %collective-permute-done.2 = bf16[2,2,512,128]{3,2,1,0:T(8,128)(2,1)S(1)} collective-permute-done((bf16[2,2,512,128]{3,2,1,0:T(8,128)(2,1)S(1)}, bf16[2,2,512,128]{3,2,1,0:T(8,128)(2,1)S(1)}, u32[]{:S(2)}, u32[]{:S(2)}) %collective-permute-start.2) | collective-permute-done | bytes 524320 | tf_op jit(solution)/shard_map/ppermute | solution.py:16
  43.9 3.9 collective-permute-done.3
  48.0 13.4 %while.19 = (s32[]{:T(128)}, bf16[2,2,512,512]{3,2,1,0:T(8,128)(2,1)S(1)}, s32[4,4]{1,0:T(4,128)S(1)}, bf16[4,2,2,256,256]{3,4,0,2,1:T(8,128)(2,1)}, s32[]{:T(128)}) while((s32[]{:T(128)}, bf16[2,2,512,512]{3,2,1,0:T(8,128)(2,1)S(1)}, s32[4,4]{1,0:T(4,128)S(1)}, bf16[4,2,2,256,256]{3,4,0,2,1:T(8,128)(2,1)}, s32[]{:T(128)}) %tuple.96), condition=%wide.while_cond.4, body=%wide.while_body.4.sunk | while | flops 2 | bytes 3145861 | solution.py:64
  61.4 2.0 convert_element_type.91
  66.3 4.0 convolution_bitcast_fusion.5
  70.3 2.9 subtract_convert_fusion.3
  73.2 3.8 convolution_bitcast_fusion.4
  77.0 3.5 subtract_convert_fusion.2
  80.5 4.3 %convolution_bitcast_fusion.3 = f32[4,2,256,256]{2,3,0,1:T(8,128)} fusion(bf16[1,2,256,256]{2,3,1,0:T(8,128)(2,1)} %get-tuple-element.208, bf16[1,2,256,256]{2,3,1,0:T(8,128)(2,1)} %get-tuple-element.209, bf16[4,1,256,256]{2,3,0,1:T(8,128)(2,1)} %get-tuple-element.179, bf16[4,1,256,256]{2,3,0,1:T(8,128)(2,1)} %get-tuple-element.178), kind=kOutput, calls=%fused_computation.23 | convolution fusion | flops 1076887552 | bytes 3670016 | tf_op jit(solution)/shard_map/nqac,pqcd->npad/dot_general | solution.py:37
  84.8 2.7 fusion.10
  87.5 4.8 %convolution_bitcast_fusion.2 = f32[4,2,256,256]{2,3,0,1:T(8,128)} fusion(bf16[1,2,256,256]{2,3,1,0:T(8,128)(2,1)} %get-tuple-element.210, bf16[1,2,256,256]{2,3,1,0:T(8,128)(2,1)} %get-tuple-element.207, f32[4,2,256,256]{2,3,0,1:T(8,128)} %convolution_bitcast_fusion.3, f32[4,256,256]{1,2,0:T(8,128)} %fusion.10), kind=kOutput, calls=%fused_computation.22 | convolution fusion | flops 1077411840 | bytes 5767168 | tf_op jit(solution)/shard_map/nqac,pqcd->npad/dot_general | solution.py:37
  92.3 4.8 %add_convert_fusion.1 = (bf16[4,1,256,256]{2,3,0,1:T(8,128)(2,1)S(1)}, bf16[4,1,256,256]{2,3,0,1:T(8,128)(2,1)}, f32[4,1,256,256]{2,3,0,1:T(8,128)}, f32[4,1,256,256]{2,3,0,1:T(8,128)}) fusion(f32[4,2,256,256]{2,3,0,1:T(8,128)} %convolution_bitcast_fusion.2, f32[4,2,256,256]{2,3,0,1:T(8,128)} %get-tuple-element.181, ...), kind=kLoop, calls=%fused_computation.62 | loop fusion | flops 3670016 | bytes 9437184 | tf_op jit(solution)/shard_map/convert.2
  97.1 3.9 convolution_bitcast_fusion.1
  101.0 2.9 add_convert_fusion
  103.8 3.9 convolution_bitcast_fusion
  107.7 3.9 multiply_add_fusion
  113.3 2.4 pad_maximum_fusion
  115.7 2.6 broadcast_in_dim.6
  118.3 79.5 %while.18 = (s32[]{:T(128)}, f32[2,2,512,512]{3,2,1,0:T(8,128)}, s32[4,2]{0,1:T(2,128)S(1)}, f32[4,2,2,256,256]{3,4,0,2,1:T(8,128)}, s32[]{:T(128)}, /*index=5*/s32[]{:T(128)}, s32[]{:T(128)}) while((s32[]{:T(128)}, f32[2,2,512,512]{3,2,1,0:T(8,128)}, s32[4,2]{0,1:T(2,128)S(1)}, f32[4,2,2,256,256]{3,4,0,2,1:T(8,128)}, s32[]{:T(128)}, ...), condition=%wide.region_1.2_spmd, body=%wide.region_0.1_spmd.sunk | while | flops 262152 | bytes 9437389 | solution.py:101
  126.2 11.9 %dynamic_update_slice.8 = f32[2,2,512,512]{3,2,1,0:T(8,128)} dynamic-update-slice(f32[2,2,512,512]{3,2,1,0:T(8,128)} %get-tuple-element.300, f32[2,2,256,256]{3,2,1,0:T(8,128)S(1)} %bitcast_add_fusion.2, s32[]{:T(128)} %constant.161.clone.1..sunk, s32[]{:T(128)} %constant.161.clone.1..sunk, s32[]{:T(128)S(6)} %select_n.100, s32[]{:T(128)S(6)} %select_n.101) | dynamic-update-slice | bytes 2097156 | tf_op jit(solution)/shard_map/while/body/eval_jaxpr/dynamic_update_slice | solution.py:99
  146.0 12.3 %dynamic_update_slice.8 = f32[2,2,512,512]{3,2,1,0:T(8,128)} dynamic-update-slice(f32[2,2,512,512]{3,2,1,0:T(8,128)} %get-tuple-element.300, f32[2,2,256,256]{3,2,1,0:T(8,128)S(1)} %bitcast_add_fusion.2, s32[]{:T(128)} %constant.161.clone.1..sunk, s32[]{:T(128)} %constant.161.clone.1..sunk, s32[]{:T(128)S(6)} %select_n.100, s32[]{:T(128)S(6)} %select_n.101) | dynamic-update-slice | bytes 2097156 | tf_op jit(solution)/shard_map/while/body/eval_jaxpr/dynamic_update_slice | solution.py:99
  166.2 11.5 %dynamic_update_slice.8 = f32[2,2,512,512]{3,2,1,0:T(8,128)} dynamic-update-slice(f32[2,2,512,512]{3,2,1,0:T(8,128)} %get-tuple-element.300, f32[2,2,256,256]{3,2,1,0:T(8,128)S(1)} %bitcast_add_fusion.2, s32[]{:T(128)} %constant.161.clone.1..sunk, s32[]{:T(128)} %constant.161.clone.1..sunk, s32[]{:T(128)S(6)} %select_n.100, s32[]{:T(128)S(6)} %select_n.101) | dynamic-update-slice | bytes 2097156 | tf_op jit(solution)/shard_map/while/body/eval_jaxpr/dynamic_update_slice | solution.py:99
  185.7 12.1 %dynamic_update_slice.8 = f32[2,2,512,512]{3,2,1,0:T(8,128)} dynamic-update-slice(f32[2,2,512,512]{3,2,1,0:T(8,128)} %get-tuple-element.300, f32[2,2,256,256]{3,2,1,0:T(8,128)S(1)} %bitcast_add_fusion.2, s32[]{:T(128)} %constant.161.clone.1..sunk, s32[]{:T(128)} %constant.161.clone.1..sunk, s32[]{:T(128)S(6)} %select_n.100, s32[]{:T(128)S(6)} %select_n.101) | dynamic-update-slice | bytes 2097156 | tf_op jit(solution)/shard_map/while/body/eval_jaxpr/dynamic_update_slice | solution.py:99
  197.8 3.2 fusion.74
  201.0 2.3 collective-permute-start.4
  205.9 17.2 %collective-permute-done.4 = f32[2,2,512,128]{3,2,1,0:T(8,128)} collective-permute-done((f32[2,2,512,128]{3,2,1,0:T(8,128)}, f32[2,2,512,128]{3,2,1,0:T(8,128)}, u32[]{:S(2)}, u32[]{:S(2)}) %collective-permute-start.4) | collective-permute-done | bytes 1048608 | tf_op jit(solution)/shard_map/ppermute | solution.py:16
  224.7 3.8 collective-permute-done.5
  231.0 6.2 %collective-permute-start.6 = (f32[2,2,128,256]{3,2,1,0:T(8,128)}, f32[2,2,128,256]{3,2,1,0:T(8,128)}, u32[]{:S(2)}, u32[]{:S(2)}) collective-permute-start(f32[2,2,128,256]{3,2,1,0:T(8,128)} %get-tuple-element.194), channel_id=1, source_target_pairs={{0,32},{32,64},{64,96},{96,128},{128,160},{160,192},{192,224},{224... | collective-permute-start | bytes 1572872 | tf_op jit(solution)/shard_map/ppermute | solution.py:16
  237.3 1.9 collective-permute-start.7
  239.2 165.7 %all-reduce.3.cloned.1.call-done = (f32[2,256,256]{1,2,0:T(8,128)}, f32[256,256]{0,1:T(8,128)}) async-done(((f32[2,256,256]{1,2,0:T(8,128)}, f32[256,256]{0,1:T(8,128)}), (f32[2,256,256]{1,2,0:T(8,128)}, f32[256,256]{0,1:T(8,128)})) %all-reduce.3.cloned.1.call-update) | async-done | bytes 786448 | tf_op jit(solution)/shard_map/psum | solution.py:153
  (131 shorter events, 64.6 us)
Async XLA Ops:
  7.2 14.5 %copy-start.17 = (f32[256,256]{1,0:T(8,128)S(1)}, f32[256,256]{1,0:T(8,128)}, u32[]{:S(2)}) copy-start(f32[256,256]{1,0:T(8,128)} %param.17) | copy-start | bytes 786436
  7.2 397.7 %all-reduce.3.cloned.1.call-start = ((), (), s32[]{:S(2)}) async-start(), calls=%async_computation | async-start | bytes 1572864 | tf_op jit(solution)/shard_map/psum | solution.py:153
  9.1 21.9 %collective-permute-start.1 = (bf16[2,2,128,256]{3,2,1,0:T(8,128)(2,1)}, bf16[2,2,128,256]{3,2,1,0:T(8,128)(2,1)}, u32[]{:S(2)}, u32[]{:S(2)}) collective-permute-start(bf16[2,2,128,256]{3,2,1,0:T(8,128)(2,1)} %get-tuple-element.203), channel_id=1, source_target_pairs={{32,0},{64,32},{96,64},{128,96},{160,128},{192,160},{224,192},{256... | collective-permute-start | bytes 786440 | tf_op jit(solution)/shard_map/ppermute | solution.py:17
  17.9 12.2 %collective-permute-start = (bf16[2,2,128,256]{3,2,1,0:T(8,128)(2,1)}, bf16[2,2,128,256]{3,2,1,0:T(8,128)(2,1)}, u32[]{:S(2)}, u32[]{:S(2)}) collective-permute-start(bf16[2,2,128,256]{3,2,1,0:T(8,128)(2,1)} %get-tuple-element.204), channel_id=1, source_target_pairs={{0,32},{32,64},{64,96},{96,128},{128,160},{160,192},{192,224},{224... | collective-permute-start | bytes 786440 | tf_op jit(solution)/shard_map/ppermute | solution.py:16
  22.7 6.1 %copy-start.16 = (f32[4,256,256]{2,1,0:T(8,128)S(1)}, f32[4,256,256]{2,1,0:T(8,128)}, u32[]{:S(2)}) copy-start(f32[4,256,256]{2,1,0:T(8,128)} %param.18) | copy-start | bytes 3145732
  26.9 4.1 copy-start.15
  32.2 11.6 %collective-permute-start.2 = (bf16[2,2,512,128]{3,2,1,0:T(8,128)(2,1)S(1)}, bf16[2,2,512,128]{3,2,1,0:T(8,128)(2,1)S(1)}, u32[]{:S(2)}, u32[]{:S(2)}) collective-permute-start(bf16[2,2,512,128]{3,2,1,0:T(8,128)(2,1)S(1)} %get-tuple-element.197), channel_id=1, source_target_pairs={{0,1},{1,2},{2,3},{3,4},{4,5},{5,6},{6,7},{7,8},{8,9},{9,10},{10,1... | collective-permute-start | bytes 1572872 | tf_op jit(solution)/shard_map/ppermute | solution.py:16
  33.6 14.2 %collective-permute-start.3 = (bf16[2,2,512,128]{3,2,1,0:T(8,128)(2,1)S(1)}, bf16[2,2,512,128]{3,2,1,0:T(8,128)(2,1)S(1)}, u32[]{:S(2)}, u32[]{:S(2)}) collective-permute-start(bf16[2,2,512,128]{3,2,1,0:T(8,128)(2,1)S(1)} %get-tuple-element.198), channel_id=1, source_target_pairs={{1,0},{2,1},{3,2},{4,3},{5,4},{6,5},{7,6},{8,7},{9,8},{10,9},{11,1... | collective-permute-start | bytes 1572872 | tf_op jit(solution)/shard_map/ppermute | solution.py:17
  63.4 1.8 copy-start.7
  63.4 1.8 copy-start.9
  66.3 4.0 copy-start.5
  70.3 2.9 copy-start.11
  70.3 2.9 copy-start.13
  80.5 4.3 %copy-start.4 = (f32[4,256,256]{1,2,0:T(8,128)S(1)}, f32[4,256,256]{1,2,0:T(8,128)}, u32[]{:S(2)}) copy-start(f32[4,256,256]{1,2,0:T(8,128)} %copy.23) | copy-start | bytes 3145732
  92.3 4.8 %copy-start.18 = (bf16[1,2,256,256]{2,3,1,0:T(8,128)(2,1)S(1)}, bf16[1,2,256,256]{2,3,1,0:T(8,128)(2,1)}, u32[]{:S(2)}) copy-start(bf16[1,2,256,256]{2,3,1,0:T(8,128)(2,1)} %get-tuple-element.208) | copy-start | bytes 786436
  97.1 3.9 copy-start.6
  101.0 2.9 copy-start.12
  101.0 2.9 copy-start.14
  103.8 3.9 copy-start.8
  111.6 1.2 copy-start.2
  111.6 1.5 copy-start.3
  115.7 2.6 copy-start.19
  197.8 6.9 %copy-start = (f32[2,2,512,512]{3,2,1,0:T(8,128)S(1)}, f32[2,2,512,512]{3,2,1,0:T(8,128)}, u32[]{:S(2)}) copy-start(f32[2,2,512,512]{3,2,1,0:T(8,128)} %get-tuple-element.129) | copy-start | bytes 12582916
  201.0 22.1 %collective-permute-start.4 = (f32[2,2,512,128]{3,2,1,0:T(8,128)}, f32[2,2,512,128]{3,2,1,0:T(8,128)}, u32[]{:S(2)}, u32[]{:S(2)}) collective-permute-start(f32[2,2,512,128]{3,2,1,0:T(8,128)} %get-tuple-element.173), channel_id=1, source_target_pairs={{0,1},{1,2},{2,3},{3,4},{4,5},{5,6},{6,7},{7,8},{8,9},{9,10},{10,1... | collective-permute-start | bytes 3145736 | tf_op jit(solution)/shard_map/ppermute | solution.py:16
  203.3 1.7 copy-start.1
  203.3 25.2 %collective-permute-start.5 = (f32[2,2,512,128]{3,2,1,0:T(8,128)}, f32[2,2,512,128]{3,2,1,0:T(8,128)}, u32[]{:S(2)}, u32[]{:S(2)}) collective-permute-start(f32[2,2,512,128]{3,2,1,0:T(8,128)} %get-tuple-element.172), channel_id=1, source_target_pairs={{1,0},{2,1},{3,2},{4,3},{5,4},{6,5},{7,6},{8,7},{9,8},{10,9},{11,1... | collective-permute-start | bytes 3145736 | tf_op jit(solution)/shard_map/ppermute | solution.py:17
  231.0 177.0 %collective-permute-start.6 = (f32[2,2,128,256]{3,2,1,0:T(8,128)}, f32[2,2,128,256]{3,2,1,0:T(8,128)}, u32[]{:S(2)}, u32[]{:S(2)}) collective-permute-start(f32[2,2,128,256]{3,2,1,0:T(8,128)} %get-tuple-element.194), channel_id=1, source_target_pairs={{0,32},{32,64},{64,96},{96,128},{128,160},{160,192},{192,224},{224... | collective-permute-start | bytes 1572872 | tf_op jit(solution)/shard_map/ppermute | solution.py:16
  237.3 171.9 %collective-permute-start.7 = (f32[2,2,128,256]{3,2,1,0:T(8,128)}, f32[2,2,128,256]{3,2,1,0:T(8,128)S(1)}, u32[]{:S(2)}, u32[]{:S(2)}) collective-permute-start(f32[2,2,128,256]{3,2,1,0:T(8,128)} %get-tuple-element.193), channel_id=1, source_target_pairs={{32,0},{64,32},{96,64},{128,96},{160,128},{192,160},{224,192},{256... | collective-permute-start | bytes 1572872 | tf_op jit(solution)/shard_map/ppermute | solution.py:17
  409.3 1.0 copy-start.10
Sparse Core Ops, SparseCore 0:
  206.0 198.7 all-reduce.2
where the time goes:
time: 420 us; the launch traced here: 417 us
  waiting for transfers between devices  198 us (47%)
  local copies, waits for them, and re-layouts  93.4 us (22%)
  other arithmetic  45.4 us (11%)
  starting transfers between devices  25.3 us (6%)
  matrix products  24.7 us (6%)
  loops' own time  15.7 us (4%)
  between operations  14.4 us (3%)
    psum x1, waiting for transfers between devices, on_device(): totals = lax.psum((probe_sum, illumination), 'row')  166 us
    dynamic_update_slice x4, local copies, waits for them, and re-layouts, place_one(): lax.dynamic_update_slice(current, present + window_gradient_stack[number]...  47.8 us
    ppermute x4, waiting for transfers between devices, extended_2(): before = lax.ppermute(last, axis, up)  24.9 us
    dot_general x6, matrix products, transform(): jnp.einsum('nqac,pqcd->npad', halfway, matrix, preferred_element_type=jnp...  24.7 us
    another operation x8, other arithmetic  18.2 us
    another operation x1, loops' own time, add_windows(): return lax.fori_loop(0, window_gradient_stack.shape[0], place_one, total)  15.6 us
    ppermute x4, starting transfers between devices, extended_2(): after = lax.ppermute(first, axis, down)  13.5 us
    gather x20, local copies, waits for them, and re-layouts  13.3 us
  transfers between devices with their start and end apart: 9, of which 5 were waited for; matrix products, arithmetic and copies ran while one was open for 5% of the time, Pallas kernels for 0%

commit v1 on v0

v1 whole, which is shorter than its diff:
```python
import functools

import jax
import jax.numpy as jnp
import numpy as np
from jax import lax
from jax.experimental import pallas as pl
from jax.experimental.pallas import tpu as pltpu
from jax.sharding import PartitionSpec as P

W = 256
H = 128
NP = 4
RC = 128
F32, BF16 = jnp.float32, jnp.bfloat16
MESH = pl.DeviceIdType.MESH
AROUND = ((-1, 0), (1, 0), (-1, -1), (-1, 1), (1, -1), (1, 1), (0, -1), (0, 1))
CHUNKS = [slice(i, i + RC) for i in range(0, W, RC)]
XS, ZS = 4, 2


def half_of(step):
    return {-1: slice(0, H), 0: slice(0, W), 1: slice(H, W)}[step]


def rim_of(step):
    return {-1: slice(3 * H, 4 * H), 0: slice(H, 3 * H), 1: slice(0, H)}[step]


def spot_of(step):
    return {-1: slice(0, H), 0: slice(H, 3 * H), 1: slice(3 * H, 4 * H)}[step]


def moved(q, by):
    return slice(q.start + by, q.stop + by)


def kernel(
    n_row, n_col,
    pos, obj, probe, phase, meas_in, cs,
    center, probe_grad,
    fwd_t, inv_t, prop, u, v, h, ext, pr, wave, g, sums, meas,
    out_row, out_col, got_row, got_col,
    core_out, core_got, x_out, x_got, z_out, z_got, fin,
    local_sem, halo_send, halo_recv, fold_send, fold_recv, sum_send, sum_recv,
):
    r, c = lax.axis_index("row"), lax.axis_index("col")
    core = lax.rem(r, 2)
    xi = lax.rem(r // 2, XS)
    zi = r // (2 * XS)

    def inside(dr, dc):
        ok = None
        for idx, step, count in ((r, dr, n_row), (c, dc, n_col)):
            if step:
                here = (idx > 0) if step < 0 else (idx < count - 1)
                ok = here if ok is None else ok & here
        return ok

    def row_at(z, x, k):
        return (z * XS + x) * 2 + k

    mates = [(row_at(zi, xi, 1 - core), c), (row_at(1 - zi, xi, core), c)]
    mates += [(row_at(zi, lax.rem(xi + d, XS), core), c) for d in range(1, XS)]

    barrier = pltpu.get_barrier_semaphore()
    for dr, dc in AROUND:
        @pl.when(inside(dr, dc))
        def _():
            pl.semaphore_signal(barrier, inc=1, device_id=(r + dr, c + dc), device_id_type=MESH)
    for mate in mates[1:]:
        pl.semaphore_signal(barrier, inc=1, device_id=mate, device_id_type=MESH)
    own = pltpu.make_async_copy(obj, ext.at[:, pl.ds(H, W), pl.ds(H, W)], local_sem.at[0])
    own.start()
    load = pltpu.make_async_copy(meas_in, meas, local_sem.at[1])
    load.start()
    peers = jnp.int32(len(mates) - 1)
    for dr, dc in AROUND:
        peers = peers + inside(dr, dc).astype(jnp.int32)
    pl.semaphore_wait(barrier, peers)

    def halo(s, k):
        dr, dc = AROUND[k]
        a, b, e, f = half_of(dr), half_of(dc), rim_of(dr), rim_of(dc)
        return pltpu.make_async_remote_copy(
            src_ref=obj.at[pl.ds(2 * s, 2), a, b],
            dst_ref=ext.at[pl.ds(2 * s, 2), e, f],
            send_sem=halo_send.at[s, k],
            recv_sem=halo_recv.at[s, k],
            device_id=(r + dr, c + dc),
            device_id_type=MESH,
        )

    def fold(s, k):
        dr, dc = AROUND[k]
        if dr:
            i = 0 if dr < 0 else 1
            place = (i, pl.ds(2 * s, 2), slice(None), spot_of(dc))
            src, dst = out_row.at[place], got_row.at[place]
        else:
            i = 0 if dc < 0 else 1
            place = (i, pl.ds(2 * s, 2))
            src, dst = out_col.at[place], got_col.at[place]
        return pltpu.make_async_remote_copy(
            src_ref=src, dst_ref=dst, send_sem=fold_send.at[s, k], recv_sem=fold_recv.at[s, k],
            device_id=(r + dr, c + dc), device_id_type=MESH,
        )

    def to_mate(src, dst, i, mate):
        return pltpu.make_async_remote_copy(
            src_ref=src, dst_ref=dst, send_sem=sum_send.at[i], recv_sem=sum_recv.at[i],
            device_id=mate, device_id_type=MESH,
        )

    def start(make, s):
        for k, (dr, dc) in enumerate(AROUND):
            @pl.when(inside(dr, dc))
            def _():
                make(s, k).start()

    def sent(make, s):
        for k, (dr, dc) in enumerate(AROUND):
            @pl.when(inside(dr, dc))
            def _():
                make(s, k).wait_send()

    def arrived(make, s):
        for k, (dr, dc) in enumerate(AROUND):
            @pl.when(inside(-dr, -dc))
            def _():
                make(s, k).wait_recv()

    start(halo, 0)
    start(halo, 1)

    for dr, dc in AROUND:
        @pl.when(jnp.logical_not(inside(-dr, -dc)))
        def _():
            e, f = rim_of(dr), rim_of(dc)
            ext[:, e, f] = jnp.zeros((4, e.stop - e.start, f.stop - f.start), BF16)

    cos_t, sin_t = cs[0], cs[1]
    for t, sgn in ((fwd_t, 1), (inv_t, -1)):
        t[0:W, 0:W] = cos_t
        t[W:, W:] = cos_t
        t[0:W, W:] = sin_t if sgn > 0 else -sin_t
        t[W:, 0:W] = -sin_t if sgn > 0 else sin_t
    for q in CHUNKS:
        prop[0, q] = jnp.cos(phase[q])
        prop[1, q] = jnp.sin(phase[q])
    sums[...] = jnp.zeros_like(sums)

    def rolled(n, _):
        for k in range(2):
            pr[n, k] = pltpu.roll(pltpu.roll(probe[k], pos[n, 0], 0), pos[n, 1], 1)
        return 0
    lax.fori_loop(0, NP, rolled, 0)

    def transform(src, lt, rt, epilogue):
        half = jnp.dot(lt[...], src, preferred_element_type=F32)
        h[:, 0:W] = half[0:W].astype(BF16)
        h[:, W:] = half[W:].astype(BF16)
        for q in CHUNKS:
            o = jnp.dot(h[q, :], rt[...], preferred_element_type=F32)
            epilogue(q, o[:, 0:W], o[:, W:])

    def put(q, re, im):
        u[q, :] = re.astype(BF16)
        u[moved(q, W), :] = im.astype(BF16)

    def picker(n):
        at, to = pos[n, 0], pos[n, 1]
        col = lax.broadcasted_iota(jnp.int32, (RC, W), 1) >= to
        row = lax.broadcasted_iota(jnp.int32, (RC, W), 0)

        def pick(plane, q):
            q2 = moved(q, W)
            a = jnp.where(col, ext[plane, q, 0:W].astype(F32), ext[plane, q, W:].astype(F32))
            b = jnp.where(col, ext[plane, q2, 0:W].astype(F32), ext[plane, q2, W:].astype(F32))
            return jnp.where(row + q.start >= at, a, b)
        return pick

    def back(x, n):
        return pltpu.roll(pltpu.roll(x, W - pos[n, 0], 0), W - pos[n, 1], 1)

    own.wait()
    arrived(halo, 0)

    def first(n, _):
        pick = picker(n)
        for q in CHUNKS:
            a, b = pick(0, q), pick(1, q)
            p, t = pr[n, 0, q], pr[n, 1, q]
            put(q, p * a - t * b, p * b + t * a)
            g[n, 0, q] = a * a + b * b
        sums[2] += back(g[n, 0], n)

        def e1(q, re, im):
            p, t = prop[0, q], prop[1, q]
            put(q, p * re - t * im, p * im + t * re)
        transform(u[...], fwd_t, inv_t, e1)

        def e2(q, re, im):
            wave[n, 0, q] = re
            wave[n, 1, q] = im
        transform(u[...], inv_t, fwd_t, e2)
        return 0
    lax.fori_loop(0, NP, first, 0)

    load.wait()
    arrived(halo, 1)

    def second(n, _):
        pick = picker(n)
        for q in CHUNKS:
            a, b = pick(2, q), pick(3, q)
            re, im = wave[n, 0, q], wave[n, 1, q]
            put(q, re * a - im * b, re * b + im * a)

        def e3(q, re, im):
            res = re * re + im * im - meas[n, q]
            put(q, res * re, res * im)
        transform(u[...], fwd_t, inv_t, e3)

        def e4(q, re, im):
            wr, wi = wave[n, 0, q], wave[n, 1, q]
            g[n, 2, q] = wr * re + wi * im
            g[n, 3, q] = wr * im - wi * re
            a, b = pick(2, q), pick(3, q)
            v[n, q] = (a * re + b * im).astype(BF16)
            v[n, moved(q, W)] = (a * im - b * re).astype(BF16)
        transform(u[...], inv_t, fwd_t, e4)
        return 0
    lax.fori_loop(0, NP, second, 0)

    def total(plane, q, a, b, cols):
        acc = None
        for n in range(NP):
            row = lax.broadcasted_iota(jnp.int32, (q.stop - q.start, H), 0) + q.start
            col = lax.broadcasted_iota(jnp.int32, (q.stop - q.start, H), 1) + cols.start
            m = (row >= pos[n, 0]) if a == 0 else (row < pos[n, 0])
            m = m & ((col >= pos[n, 1]) if b == 0 else (col < pos[n, 1]))
            part = jnp.where(m, g[n, plane, q, cols], 0.0)
            acc = part if acc is None else acc + part
        return acc

    lo, hi = slice(0, H), slice(H, W)

    def outer(plane, _):
        for j in range(4):
            out_row[0, plane, :, j * H:(j + 1) * H] = total(plane, lo, 0, j // 2, (lo, hi)[j % 2]).astype(BF16)
            out_row[1, plane, :, j * H:(j + 1) * H] = total(plane, hi, 1, j // 2, (lo, hi)[j % 2]).astype(BF16)
        for i, q in enumerate((hi, lo)):
            rows = slice(i * H, (i + 1) * H)
            out_col[0, plane, rows] = total(plane, q, i, 0, lo).astype(BF16)
            out_col[1, plane, rows] = total(plane, q, i, 1, hi).astype(BF16)
        return 0

    def inner(plane, _):
        for i, q in enumerate((hi, lo)):
            rows = slice(i * H, (i + 1) * H)
            center[plane, rows, 0:H] = total(plane, q, i, 0, hi)
            center[plane, rows, H:] = total(plane, q, i, 1, lo)
        return 0

    def add_fold(s, k):
        dr, dc = AROUND[k]
        e = half_of(-dr)
        f = half_of(-dc)

        @pl.when(inside(-dr, -dc))
        def _():
            fold(s, k).wait_recv()
            for plane in (2 * s, 2 * s + 1):
                if dr:
                    got = got_row[0 if dr < 0 else 1, plane, :, spot_of(dc)]
                else:
                    got = got_col[0 if dc < 0 else 1, plane]
                center[plane, e, f] += got.astype(F32)

    lax.fori_loop(2, 4, outer, 0)
    start(fold, 1)

    def third(n, _):
        def e5(q, re, im):
            p, t = prop[0, q], prop[1, q]
            put(q, p * re + t * im, p * im - t * re)
        transform(v[n], fwd_t, inv_t, e5)
        pick = picker(n)

        def e6(q, re, im):
            p, t = pr[n, 0, q], pr[n, 1, q]
            g[n, 0, q] = p * re + t * im
            g[n, 1, q] = p * im - t * re
            a, b = pick(0, q), pick(1, q)
            wave[n, 0, q] = a * re + b * im
            wave[n, 1, q] = a * im - b * re
        transform(u[...], inv_t, fwd_t, e6)
        sums[0] += back(wave[n, 0], n)
        sums[1] += back(wave[n, 1], n)
        return 0
    lax.fori_loop(0, NP, third, 0)

    mine = pl.ds(pl.multiple_of(core * H, H), H)
    other = pl.ds(pl.multiple_of((1 - core) * H, H), H)
    core_out[...] = sums[:, other].astype(BF16)
    swap = to_mate(core_out, core_got, 0, mates[0])
    swap.start()
    lax.fori_loop(0, 2, outer, 0)
    start(fold, 0)

    Q = H // XS
    swap.wait()
    sums[:, mine] = sums[:, mine] + core_got[...].astype(F32)
    spread = []
    for d in range(1, XS):
        at = pl.multiple_of(core * H + lax.rem(xi + d, XS) * Q, Q)
        x_out[d - 1] = sums[:, pl.ds(at, Q)].astype(BF16)
        cp = to_mate(x_out.at[d - 1], x_got.at[d - 1], d, mates[1 + d])
        cp.start()
        spread.append(cp)
    lax.fori_loop(2, 4, inner, 0)
    lax.fori_loop(0, 2, inner, 0)
    acc = sums[:, pl.ds(pl.multiple_of(core * H + xi * Q, Q), Q)]
    for d in range(1, XS):
        spread[d - 1].wait()
        acc = acc + x_got[d - 1].astype(F32)
    z_out[...] = acc.astype(BF16)
    cross = to_mate(z_out, z_got, XS, mates[1])
    cross.start()
    for k in range(8):
        add_fold(1, k)
    cross.wait()
    tot = z_out[...].astype(F32) + z_got[...].astype(F32)
    scale = 1.0 / jnp.sqrt(tot[2] + 1e-06)
    here = pl.ds(pl.multiple_of(core * H + xi * Q, Q), Q)
    fin[0, here] = (tot[0] * scale).astype(BF16)
    fin[1, here] = (tot[1] * scale).astype(BF16)
    gather = []
    for d in range(1, XS):
        cp = to_mate(fin.at[:, here], fin.at[:, here], XS + d, mates[1 + d])
        cp.start()
        gather.append(cp)
    for d in range(1, XS):
        gather[d - 1].wait()
    last = to_mate(fin.at[:, mine], fin.at[:, mine], 2 * XS, mates[0])
    last.start()
    for k in (6, 7, 0, 1, 2, 3, 4, 5):
        add_fold(0, k)
    last.wait()
    probe_grad[...] = fin[...].astype(F32)
    for s in range(2):
        sent(halo, s)
        sent(fold, s)


def tables():
    k = np.arange(W)
    ang = 2.0 * np.pi * ((k[:, None] * k[None, :]) % W) / W
    both = np.stack([np.cos(ang), np.sin(ang)]) / np.sqrt(W)
    return jnp.asarray(both.astype(np.float32)).astype(BF16)


def on_device(n_row, n_col, object_slices, probe_wave_parts, prop_phase, measured, positions):
    vm = pl.BlockSpec(memory_space=pltpu.VMEM)
    anys = pl.BlockSpec(memory_space=pl.ANY)
    shape = jax.ShapeDtypeStruct
    Q = H // XS
    dma = pltpu.SemaphoreType.DMA
    center, probe_grad = pl.pallas_call(
        functools.partial(kernel, n_row, n_col),
        out_shape=(shape((4, W, W), F32), shape((2, W, W), F32)),
        in_specs=[pl.BlockSpec(memory_space=pltpu.SMEM), anys, vm, vm, anys, vm],
        out_specs=(vm, vm),
        scratch_shapes=[
            pltpu.VMEM((2 * W, 2 * W), BF16), pltpu.VMEM((2 * W, 2 * W), BF16), pltpu.VMEM((2, W, W), F32),
            pltpu.VMEM((2 * W, W), BF16), pltpu.VMEM((NP, 2 * W, W), BF16), pltpu.VMEM((W, 2 * W), BF16),
            pltpu.VMEM((4, 2 * W, 2 * W), BF16), pltpu.VMEM((NP, 2, W, W), F32), pltpu.VMEM((NP, 2, W, W), F32),
            pltpu.VMEM((NP, 4, W, W), F32), pltpu.VMEM((3, W, W), F32), pltpu.VMEM((NP, W, W), F32),
            pltpu.VMEM((2, 4, H, 2 * W), BF16), pltpu.VMEM((2, 4, W, H), BF16),
            pltpu.VMEM((2, 4, H, 2 * W), BF16), pltpu.VMEM((2, 4, W, H), BF16),
            pltpu.VMEM((3, H, W), BF16), pltpu.VMEM((3, H, W), BF16),
            pltpu.VMEM((XS - 1, 3, Q, W), BF16), pltpu.VMEM((XS - 1, 3, Q, W), BF16),
            pltpu.VMEM((3, Q, W), BF16), pltpu.VMEM((3, Q, W), BF16), pltpu.VMEM((2, W, W), BF16),
            dma((2,)), dma((2, 8)), dma((2, 8)), dma((2, 8)), dma((2, 8)), dma((2 * XS + 1,)), dma((2 * XS + 1,)),
        ],
        compiler_params=pltpu.CompilerParams(collective_id=0, has_side_effects=True, vmem_limit_bytes=60 << 20),
    )(positions, object_slices.reshape(4, W, W), probe_wave_parts[0], prop_phase, measured, tables())
    return center.reshape(2, 2, W, W), probe_grad[None]


def solution(mesh):
    return jax.shard_map(
        functools.partial(on_device, mesh.shape["row"], mesh.shape["col"]),
        mesh=mesh,
        in_specs=(
            P(None, None, "row", "col"),
            P("col", None, None, None),
            P(),
            P(("row", "col"), None, None),
            P(("row", "col"), None),
        ),
        out_specs=(P(None, None, "row", "col"), P("col", None, None, None)),
        check_vma=False,
    )
```

time: 420 us -> 77.6 us (0.18)
  the two profiles are of different devices: /device:TPU:1 before, /device:TPU:129 now
where the time goes in v1:
time: 77.6 us; the launch traced here: 77.4 us
  Pallas kernels  72.3 us (93%)
  local copies, waits for them, and re-layouts  4.48 us (6%)
    pallas_call x1, Pallas kernels, on_device(): pl.pallas_call(functools.partial(kernel, n_row, n_col), out_shape=(shape(...  72.3 us
    unnamed x7, local copies, waits for them, and re-layouts  4.48 us

profile of v1, /device:TPU:129, one launch (start us, length us, event | category | flops | bytes accessed | tf_op | source)
XLA Modules:
  0.0 77.4 jit_solution(4225479563588661995)
XLA Ops:
  0.6 0.0 copy-start.1
  0.6 0.7 copy-done.1
  1.3 0.7 copy.8.pos
  2.0 72.3 %shard_map.77 = (f32[4,256,256]{2,1,0:T(8,128)}, f32[2,256,256]{2,1,0:T(8,128)}) custom-call(s32[4,2]{1,0:T(4,128)} %copy.8.pos, bf16[4,256,256]{2,1,0:T(8,128)(2,1)} %bitcast.6, f32[2,256,256]{2,1,0:T(8,128)} %bitcast.7, f32[256,256]{1,0:T(8,128)} %phase.1, f32[4,256,256]{2,1,0:T(8,128)} %meas_in.1, bf16[2,256,256]{2,1,0:T(8,128)(2,1)} %constant.6.cs), custom_call_target="tpu_custom_call" | custom-call | tf_op jit(solution)/shard_map/pallas_call | solution.py:370
  74.3 0.0 copy-start
  74.3 2.3 %copy.11 = f32[2,2,256,256]{3,2,1,0:T(8,128)} copy(f32[2,2,256,256]{3,2,1,0:T(8,128)} %bitcast.4) | data formatting | bytes 2097152
  76.6 0.0 copy-done
  76.6 0.8 %copy.12 = f32[1,2,256,256]{3,2,1,0:T(8,128)} copy(f32[1,2,256,256]{3,2,1,0:T(8,128)S(1)} %bitcast.5) | data formatting | bytes 1048576
Async XLA Ops:
  0.6 0.7 copy-start.1
  74.3 2.4 %copy-start = (f32[2,256,256]{2,1,0:T(8,128)S(1)}, f32[2,256,256]{2,1,0:T(8,128)}, u32[]{:S(2)}) copy-start(f32[2,256,256]{2,1,0:T(8,128)} %get-tuple-element.5) | copy-start | bytes 1572868

commit v2 on v1

--- a/solution.py
+++ b/solution.py
@@ -12,6 +12,7 @@
 H = 128
 NP = 4
 RC = 128
+UNROLL = 4
 F32, BF16 = jnp.float32, jnp.bfloat16
 MESH = pl.DeviceIdType.MESH
 AROUND = ((-1, 0), (1, 0), (-1, -1), (-1, 1), (1, -1), (1, 1), (0, -1), (0, 1))
@@ -38,10 +39,10 @@
 def kernel(
     n_row, n_col,
     pos, obj, probe, phase, meas_in, cs,
-    center, probe_grad,
+    grad, fin,
     fwd_t, inv_t, prop, u, v, h, ext, pr, wave, g, sums, meas,
     out_row, out_col, got_row, got_col,
-    core_out, core_got, x_out, x_got, z_out, z_got, fin,
+    core_out, core_got, x_out, x_got, z_out, z_got, center,
     local_sem, halo_send, halo_recv, fold_send, fold_recv, sum_send, sum_recv,
 ):
     r, c = lax.axis_index("row"), lax.axis_index("col")
@@ -152,94 +153,97 @@
 
     def rolled(n, _):
         for k in range(2):
-            pr[n, k] = pltpu.roll(pltpu.roll(probe[k], pos[n, 0], 0), pos[n, 1], 1)
+            pr[n, k] = pltpu.roll(pltpu.roll(probe[k], pos[0, n], 0), pos[1, n], 1)
         return 0
     lax.fori_loop(0, NP, rolled, 0)
 
     def transform(src, lt, rt, epilogue):
-        half = jnp.dot(lt[...], src, preferred_element_type=F32)
-        h[:, 0:W] = half[0:W].astype(BF16)
-        h[:, W:] = half[W:].astype(BF16)
-        for q in CHUNKS:
-            o = jnp.dot(h[q, :], rt[...], preferred_element_type=F32)
-            epilogue(q, o[:, 0:W], o[:, W:])
-
-    def put(q, re, im):
-        u[q, :] = re.astype(BF16)
-        u[moved(q, W), :] = im.astype(BF16)
-
-    def picker(n):
-        at, to = pos[n, 0], pos[n, 1]
-        col = lax.broadcasted_iota(jnp.int32, (RC, W), 1) >= to
-        row = lax.broadcasted_iota(jnp.int32, (RC, W), 0)
-
-        def pick(plane, q):
-            q2 = moved(q, W)
-            a = jnp.where(col, ext[plane, q, 0:W].astype(F32), ext[plane, q, W:].astype(F32))
-            b = jnp.where(col, ext[plane, q2, 0:W].astype(F32), ext[plane, q2, W:].astype(F32))
-            return jnp.where(row + q.start >= at, a, b)
-        return pick
+        def run(n):
+            half = jnp.dot(lt[...], src[n], preferred_element_type=F32)
+            h[n, :, 0:W] = half[0:W].astype(BF16)
+            h[n, :, W:] = half[W:].astype(BF16)
+            for q in CHUNKS:
+                o = jnp.dot(h[n, q, :], rt[...], preferred_element_type=F32)
+                epilogue(n, q, o[:, 0:W], o[:, W:])
+        return run
+
+    def put(n, q, re, im):
+        u[n, q, :] = re.astype(BF16)
+        u[n, moved(q, W), :] = im.astype(BF16)
+
+    def pick(n, plane, q):
+        col = lax.broadcasted_iota(jnp.int32, (RC, W), 1) >= pos[1, n]
+        row = lax.broadcasted_iota(jnp.int32, (RC, W), 0) + q.start >= pos[0, n]
+        q2 = moved(q, W)
+        a = jnp.where(col, ext[plane, q, 0:W].astype(F32), ext[plane, q, W:].astype(F32))
+        b = jnp.where(col, ext[plane, q2, 0:W].astype(F32), ext[plane, q2, W:].astype(F32))
+        return jnp.where(row, a, b)
+
+    def sweep(*stages):
+        def some(i, _):
+            for stage in stages:
+                for k in range(UNROLL):
+                    stage(i * UNROLL + k)
+            return 0
+        if UNROLL == NP:
+            some(0, 0)
+        else:
+            lax.fori_loop(0, NP // UNROLL, some, 0)
 
     def back(x, n):
-        return pltpu.roll(pltpu.roll(x, W - pos[n, 0], 0), W - pos[n, 1], 1)
+        return pltpu.roll(pltpu.roll(x, W - pos[0, n], 0), W - pos[1, n], 1)
 
     own.wait()
     arrived(halo, 0)
 
-    def first(n, _):
-        pick = picker(n)
+    def first_exit(n):
         for q in CHUNKS:
-            a, b = pick(0, q), pick(1, q)
+            a, b = pick(n, 0, q), pick(n, 1, q)
             p, t = pr[n, 0, q], pr[n, 1, q]
-            put(q, p * a - t * b, p * b + t * a)
+            put(n, q, p * a - t * b, p * b + t * a)
             g[n, 0, q] = a * a + b * b
+
+    def bright(n):
         sums[2] += back(g[n, 0], n)
 
-        def e1(q, re, im):
-            p, t = prop[0, q], prop[1, q]
-            put(q, p * re - t * im, p * im + t * re)
-        transform(u[...], fwd_t, inv_t, e1)
-
-        def e2(q, re, im):
-            wave[n, 0, q] = re
-            wave[n, 1, q] = im
-        transform(u[...], inv_t, fwd_t, e2)
-        return 0
-    lax.fori_loop(0, NP, first, 0)
+    def e1(n, q, re, im):
+        p, t = prop[0, q], prop[1, q]
+        put(n, q, p * re - t * im, p * im + t * re)
+
+    def e2(n, q, re, im):
+        wave[n, 0, q] = re
+        wave[n, 1, q] = im
+    sweep(first_exit, bright, transform(u, fwd_t, inv_t, e1), transform(u, inv_t, fwd_t, e2))
 
     load.wait()
     arrived(halo, 1)
 
-    def second(n, _):
-        pick = picker(n)
+    def second_exit(n):
         for q in CHUNKS:
-            a, b = pick(2, q), pick(3, q)
+            a, b = pick(n, 2, q), pick(n, 3, q)
             re, im = wave[n, 0, q], wave[n, 1, q]
-            put(q, re * a - im * b, re * b + im * a)
-
-        def e3(q, re, im):
-            res = re * re + im * im - meas[n, q]
-            put(q, res * re, res * im)
-        transform(u[...], fwd_t, inv_t, e3)
-
-        def e4(q, re, im):
-            wr, wi = wave[n, 0, q], wave[n, 1, q]
-            g[n, 2, q] = wr * re + wi * im
-            g[n, 3, q] = wr * im - wi * re
-            a, b = pick(2, q), pick(3, q)
-            v[n, q] = (a * re + b * im).astype(BF16)
-            v[n, moved(q, W)] = (a * im - b * re).astype(BF16)
-        transform(u[...], inv_t, fwd_t, e4)
-        return 0
-    lax.fori_loop(0, NP, second, 0)
+            put(n, q, re * a - im * b, re * b + im * a)
+
+    def e3(n, q, re, im):
+        res = re * re + im * im - meas[n, q]
+        put(n, q, res * re, res * im)
+
+    def e4(n, q, re, im):
+        wr, wi = wave[n, 0, q], wave[n, 1, q]
+        g[n, 2, q] = wr * re + wi * im
+        g[n, 3, q] = wr * im - wi * re
+        a, b = pick(n, 2, q), pick(n, 3, q)
+        v[n, q] = (a * re + b * im).astype(BF16)
+        v[n, moved(q, W)] = (a * im - b * re).astype(BF16)
+    sweep(second_exit, transform(u, fwd_t, inv_t, e3), transform(u, inv_t, fwd_t, e4))
 
     def total(plane, q, a, b, cols):
         acc = None
         for n in range(NP):
             row = lax.broadcasted_iota(jnp.int32, (q.stop - q.start, H), 0) + q.start
             col = lax.broadcasted_iota(jnp.int32, (q.stop - q.start, H), 1) + cols.start
-            m = (row >= pos[n, 0]) if a == 0 else (row < pos[n, 0])
-            m = m & ((col >= pos[n, 1]) if b == 0 else (col < pos[n, 1]))
+            m = (row >= pos[0, n]) if a == 0 else (row < pos[0, n])
+            m = m & ((col >= pos[1, n]) if b == 0 else (col < pos[1, n]))
             part = jnp.where(m, g[n, plane, q, cols], 0.0)
             acc = part if acc is None else acc + part
         return acc
@@ -281,25 +285,24 @@
     lax.fori_loop(2, 4, outer, 0)
     start(fold, 1)
 
-    def third(n, _):
-        def e5(q, re, im):
-            p, t = prop[0, q], prop[1, q]
-            put(q, p * re + t * im, p * im - t * re)
-        transform(v[n], fwd_t, inv_t, e5)
-        pick = picker(n)
-
-        def e6(q, re, im):
-            p, t = pr[n, 0, q], pr[n, 1, q]
-            g[n, 0, q] = p * re + t * im
-            g[n, 1, q] = p * im - t * re
-            a, b = pick(0, q), pick(1, q)
-            wave[n, 0, q] = a * re + b * im
-            wave[n, 1, q] = a * im - b * re
-        transform(u[...], inv_t, fwd_t, e6)
+    lax.fori_loop(2, 4, inner, 0)
+
+    def e5(n, q, re, im):
+        p, t = prop[0, q], prop[1, q]
+        put(n, q, p * re + t * im, p * im - t * re)
+
+    def e6(n, q, re, im):
+        p, t = pr[n, 0, q], pr[n, 1, q]
+        g[n, 0, q] = p * re + t * im
+        g[n, 1, q] = p * im - t * re
+        a, b = pick(n, 0, q), pick(n, 1, q)
+        wave[n, 0, q] = a * re + b * im
+        wave[n, 1, q] = a * im - b * re
+
+    def probe_back(n):
         sums[0] += back(wave[n, 0], n)
         sums[1] += back(wave[n, 1], n)
-        return 0
-    lax.fori_loop(0, NP, third, 0)
+    sweep(transform(v, fwd_t, inv_t, e5), transform(u, inv_t, fwd_t, e6), probe_back)
 
     mine = pl.ds(pl.multiple_of(core * H, H), H)
     other = pl.ds(pl.multiple_of((1 - core) * H, H), H)
@@ -319,7 +322,6 @@
         cp = to_mate(x_out.at[d - 1], x_got.at[d - 1], d, mates[1 + d])
         cp.start()
         spread.append(cp)
-    lax.fori_loop(2, 4, inner, 0)
     lax.fori_loop(0, 2, inner, 0)
     acc = sums[:, pl.ds(pl.multiple_of(core * H + xi * Q, Q), Q)]
     for d in range(1, XS):
@@ -348,7 +350,8 @@
     for k in (6, 7, 0, 1, 2, 3, 4, 5):
         add_fold(0, k)
     last.wait()
-    probe_grad[...] = fin[...].astype(F32)
+    for k in range(4):
+        grad[k] = center[k].astype(BF16)
     for s in range(2):
         sent(halo, s)
         sent(fold, s)
@@ -367,26 +370,26 @@
     shape = jax.ShapeDtypeStruct
     Q = H // XS
     dma = pltpu.SemaphoreType.DMA
-    center, probe_grad = pl.pallas_call(
+    grad, probe_grad = pl.pallas_call(
         functools.partial(kernel, n_row, n_col),
-        out_shape=(shape((4, W, W), F32), shape((2, W, W), F32)),
+        out_shape=(shape((4, W, W), BF16), shape((2, W, W), BF16)),
         in_specs=[pl.BlockSpec(memory_space=pltpu.SMEM), anys, vm, vm, anys, vm],
         out_specs=(vm, vm),
         scratch_shapes=[
             pltpu.VMEM((2 * W, 2 * W), BF16), pltpu.VMEM((2 * W, 2 * W), BF16), pltpu.VMEM((2, W, W), F32),
-            pltpu.VMEM((2 * W, W), BF16), pltpu.VMEM((NP, 2 * W, W), BF16), pltpu.VMEM((W, 2 * W), BF16),
+            pltpu.VMEM((NP, 2 * W, W), BF16), pltpu.VMEM((NP, 2 * W, W), BF16), pltpu.VMEM((NP, W, 2 * W), BF16),
             pltpu.VMEM((4, 2 * W, 2 * W), BF16), pltpu.VMEM((NP, 2, W, W), F32), pltpu.VMEM((NP, 2, W, W), F32),
             pltpu.VMEM((NP, 4, W, W), F32), pltpu.VMEM((3, W, W), F32), pltpu.VMEM((NP, W, W), F32),
             pltpu.VMEM((2, 4, H, 2 * W), BF16), pltpu.VMEM((2, 4, W, H), BF16),
             pltpu.VMEM((2, 4, H, 2 * W), BF16), pltpu.VMEM((2, 4, W, H), BF16),
             pltpu.VMEM((3, H, W), BF16), pltpu.VMEM((3, H, W), BF16),
             pltpu.VMEM((XS - 1, 3, Q, W), BF16), pltpu.VMEM((XS - 1, 3, Q, W), BF16),
-            pltpu.VMEM((3, Q, W), BF16), pltpu.VMEM((3, Q, W), BF16), pltpu.VMEM((2, W, W), BF16),
+            pltpu.VMEM((3, Q, W), BF16), pltpu.VMEM((3, Q, W), BF16), pltpu.VMEM((4, W, W), F32),
             dma((2,)), dma((2, 8)), dma((2, 8)), dma((2, 8)), dma((2, 8)), dma((2 * XS + 1,)), dma((2 * XS + 1,)),
         ],
         compiler_params=pltpu.CompilerParams(collective_id=0, has_side_effects=True, vmem_limit_bytes=60 << 20),
-    )(positions, object_slices.reshape(4, W, W), probe_wave_parts[0], prop_phase, measured, tables())
-    return center.reshape(2, 2, W, W), probe_grad[None]
+    )(positions.T, object_slices.reshape(4, W, W), probe_wave_parts[0], prop_phase, measured, tables())
+    return grad.reshape(2, 2, W, W).astype(F32), probe_grad[None].astype(F32)
 
 
 def solution(mesh):

time: 77.6 us -> 68.7 us (0.89)
  Pallas kernels: 72.3 us -> 64.9 us
  local copies, waits for them, and re-layouts: 4.48 us -> 0.01 us
  other arithmetic: 0 us -> 2.97 us
    pallas_call x1, Pallas kernels: 72.3 us -> 64.9 us  [on_device(): pl.pallas_call(functools.partial(kernel, n_row, n_col), out_shape=(shape(...]
    unnamed x7 -> x2, local copies, waits for them, and re-layouts: 4.48 us -> 0.01 us
    convert_element_type x0 -> x2, other arithmetic: none -> 2.97 us  [on_device(): return (grad.reshape(2, 2, W, W).astype(F32), probe_grad[None].astype(F32))]
where the time goes in v2:
time: 68.7 us; the launch traced here: 68.5 us
  Pallas kernels  64.9 us (94%)
  other arithmetic  2.97 us (4%)
    pallas_call x1, Pallas kernels, on_device(): pl.pallas_call(functools.partial(kernel, n_row, n_col), out_shape=(shape(...  64.9 us
    convert_element_type x2, other arithmetic, on_device(): return (grad.reshape(2, 2, W, W).astype(F32), probe_grad[None].astype(F32))  2.97 us

profile of v2, /device:TPU:129, one launch (start us, length us, event | category | flops | bytes accessed | tf_op | source)
XLA Modules:
  0.0 68.5 jit_solution(4125287947277079498)
XLA Ops:
  0.6 64.9 %shard_map.77 = (bf16[4,256,256]{2,1,0:T(8,128)(2,1)}, bf16[2,256,256]{2,1,0:T(8,128)(2,1)}) custom-call(s32[2,4]{1,0:T(2,128)} %bitcast.11, bf16[4,256,256]{2,1,0:T(8,128)(2,1)} %bitcast.8, f32[2,256,256]{2,1,0:T(8,128)} %bitcast.9, f32[256,256]{1,0:T(8,128)} %phase.1, f32[4,256,256]{2,1,0:T(8,128)} %meas_in.1, bf16[2,256,256]{2,1,0:T(8,128)(2,1)} %constant.6.cs), custom_call_target="tpu_custom_call" | custom-call | tf_op jit(solution)/shard_map/pallas_call | solution.py:373
  65.6 0.0 copy-start
  65.6 2.1 %convert.2 = f32[2,2,256,256]{3,2,1,0:T(8,128)} convert(bf16[2,2,256,256]{3,2,1,0:T(8,128)(2,1)} %bitcast.10) | non-fusion elementwise | flops 262144 | bytes 1572864 | tf_op jit(solution)/shard_map/convert_element_type | solution.py:392
  67.7 0.0 copy-done
  67.7 0.8 %bitcast_convert_fusion = f32[1,2,256,256]{3,2,1,0:T(8,128)} fusion(bf16[2,256,256]{2,1,0:T(8,128)(2,1)S(1)} %copy-done), kind=kLoop, calls=%fused_computation | loop fusion | flops 131072 | bytes 786432 | tf_op jit(solution)/shard_map/convert_element_type | solution.py:392
Async XLA Ops:
  65.6 2.2 %copy-start = (bf16[2,256,256]{2,1,0:T(8,128)(2,1)S(1)}, bf16[2,256,256]{2,1,0:T(8,128)(2,1)}, u32[]{:S(2)}) copy-start(bf16[2,256,256]{2,1,0:T(8,128)(2,1)} %get-tuple-element.5) | copy-start | bytes 786436

commit v3 on v2

--- a/solution.py
+++ b/solution.py
@@ -18,6 +18,8 @@
 AROUND = ((-1, 0), (1, 0), (-1, -1), (-1, 1), (1, -1), (1, 1), (0, -1), (0, 1))
 CHUNKS = [slice(i, i + RC) for i in range(0, W, RC)]
 XS, ZS = 4, 2
+LOOP = 8
+TURNS = [(dr, dc) for dc in (-1, 1) for dr in (-1, 1)]
 
 
 def half_of(step):
@@ -43,7 +45,7 @@
     fwd_t, inv_t, prop, u, v, h, ext, pr, wave, g, sums, meas,
     out_row, out_col, got_row, got_col,
     core_out, core_got, x_out, x_got, z_out, z_got, center,
-    local_sem, halo_send, halo_recv, fold_send, fold_recv, sum_send, sum_recv,
+    turned, local_sem, turn_send, turn_recv, halo_send, halo_recv, fold_send, fold_recv, sum_send, sum_recv,
 ):
     r, c = lax.axis_index("row"), lax.axis_index("col")
     core = lax.rem(r, 2)
@@ -57,6 +59,25 @@
                 here = (idx > 0) if step < 0 else (idx < count - 1)
                 ok = here if ok is None else ok & here
         return ok
+
+    def col_far(at, step):
+        return lax.rem(at, LOOP) == (LOOP - 1 if step > 0 else 0)
+
+    def row_far(at, step):
+        return at == (n_row // ZS - 1 if step > 0 else n_row // ZS)
+
+    def bent(row, col, dr, dc):
+        return col_far(col, dc) & jnp.logical_not(row_far(row, dr))
+
+    def leaves(k):
+        dr, dc = AROUND[k]
+        ok = inside(dr, dc)
+        return ok & jnp.logical_not(bent(r, c, dr, dc)) if dr and dc else ok
+
+    def lands(k):
+        dr, dc = AROUND[k]
+        ok = inside(-dr, -dc)
+        return ok & jnp.logical_not(bent(r - dr, c - dc, dr, dc)) if dr and dc else ok
 
     def row_at(z, x, k):
         return (z * XS + x) * 2 + k
@@ -113,26 +134,107 @@
             device_id=mate, device_id_type=MESH,
         )
 
-    def start(make, s):
+    def pass_on(s, t):
+        dr, dc = TURNS[t]
+        e, f = half_of(dr), rim_of(dc)
+        return pltpu.make_async_remote_copy(
+            src_ref=ext.at[pl.ds(2 * s, 2), moved(e, H), f],
+            dst_ref=ext.at[pl.ds(2 * s, 2), rim_of(dr), f],
+            send_sem=turn_send.at[s, t],
+            recv_sem=halo_recv.at[s, AROUND.index((dr, dc))],
+            device_id=(r + dr, c),
+            device_id_type=MESH,
+        )
+
+    def turn(s, t):
+        dr, dc = TURNS[t]
+        k = AROUND.index((dr, dc))
+        place = (0 if dr < 0 else 1, pl.ds(2 * s, 2), slice(None), spot_of(dc))
+        return pltpu.make_async_remote_copy(
+            src_ref=out_row.at[place], dst_ref=turned.at[s, t], send_sem=fold_send.at[s, k], recv_sem=turn_recv.at[s, t],
+            device_id=(r + dr, c), device_id_type=MESH,
+        )
+
+    def passes(t):
+        dr, dc = TURNS[t]
+        return inside(0, -dc) & inside(dr, 0) & bent(r, c - dc, dr, dc)
+
+    def gets(t):
+        dr, dc = TURNS[t]
+        return inside(0, dc) & inside(-dr, 0) & bent(r - dr, c, dr, dc)
+
+    def halo_start(s):
+        for k in range(8):
+            @pl.when(leaves(k))
+            def _():
+                halo(s, k).start()
+
+    def halo_turn(s):
+        for dc in (-1, 1):
+            @pl.when(inside(0, -dc) & col_far(c - dc, dc))
+            def _():
+                halo(s, AROUND.index((0, dc))).wait_recv()
+        for t in range(4):
+            @pl.when(passes(t))
+            def _():
+                pass_on(s, t).start()
+
+    def halo_arrived(s):
+        for k, (dr, dc) in enumerate(AROUND):
+            ok = inside(-dr, -dc)
+            if not dr:
+                ok = ok & jnp.logical_not(col_far(c - dc, dc))
+
+            @pl.when(ok)
+            def _():
+                halo(s, k).wait_recv()
+
+    def halo_sent(s):
+        for k in range(8):
+            @pl.when(leaves(k))
+            def _():
+                halo(s, k).wait_send()
+        for t in range(4):
+            @pl.when(passes(t))
+            def _():
+                pass_on(s, t).wait_send()
+
+    def fold_start(s):
+        for k, (dr, dc) in enumerate(AROUND):
+            ok = leaves(k)
+            if not dr:
+                ok = ok & jnp.logical_not(col_far(c, dc))
+            elif dc:
+                @pl.when(inside(dr, dc) & bent(r, c, dr, dc))
+                def _():
+                    turn(s, TURNS.index((dr, dc))).start()
+
+            @pl.when(ok)
+            def _():
+                fold(s, k).start()
+
+    def fold_turn(s):
+        for t, (dr, dc) in enumerate(TURNS):
+            @pl.when(gets(t))
+            def _():
+                turn(s, t).wait_recv()
+                rows = half_of(-dr)
+                for p in range(2):
+                    i = (0 if dc < 0 else 1, 2 * s + p, rows)
+                    out_col[i] = (out_col[i].astype(F32) + turned[s, t, p].astype(F32)).astype(BF16)
+        for dc in (-1, 1):
+            @pl.when(inside(0, dc) & col_far(c, dc))
+            def _():
+                fold(s, AROUND.index((0, dc))).start()
+
+    def fold_sent(s):
         for k, (dr, dc) in enumerate(AROUND):
             @pl.when(inside(dr, dc))
             def _():
-                make(s, k).start()
-
-    def sent(make, s):
-        for k, (dr, dc) in enumerate(AROUND):
-            @pl.when(inside(dr, dc))
-            def _():
-                make(s, k).wait_send()
-
-    def arrived(make, s):
-        for k, (dr, dc) in enumerate(AROUND):
-            @pl.when(inside(-dr, -dc))
-            def _():
-                make(s, k).wait_recv()
-
-    start(halo, 0)
-    start(halo, 1)
+                fold(s, k).wait_send()
+
+    halo_start(0)
+    halo_start(1)
 
     for dr, dc in AROUND:
         @pl.when(jnp.logical_not(inside(-dr, -dc)))
@@ -193,8 +295,9 @@
     def back(x, n):
         return pltpu.roll(pltpu.roll(x, W - pos[0, n], 0), W - pos[1, n], 1)
 
+    halo_turn(0)
     own.wait()
-    arrived(halo, 0)
+    halo_arrived(0)
 
     def first_exit(n):
         for q in CHUNKS:
@@ -213,10 +316,12 @@
     def e2(n, q, re, im):
         wave[n, 0, q] = re
         wave[n, 1, q] = im
-    sweep(first_exit, bright, transform(u, fwd_t, inv_t, e1), transform(u, inv_t, fwd_t, e2))
+    sweep(first_exit, bright, transform(u, fwd_t, inv_t, e1))
+    halo_turn(1)
+    sweep(transform(u, inv_t, fwd_t, e2))
 
     load.wait()
-    arrived(halo, 1)
+    halo_arrived(1)
 
     def second_exit(n):
         for q in CHUNKS:
@@ -272,7 +377,7 @@
         e = half_of(-dr)
         f = half_of(-dc)
 
-        @pl.when(inside(-dr, -dc))
+        @pl.when(lands(k))
         def _():
             fold(s, k).wait_recv()
             for plane in (2 * s, 2 * s + 1):
@@ -283,7 +388,7 @@
                 center[plane, e, f] += got.astype(F32)
 
     lax.fori_loop(2, 4, outer, 0)
-    start(fold, 1)
+    fold_start(1)
 
     lax.fori_loop(2, 4, inner, 0)
 
@@ -309,8 +414,9 @@
     core_out[...] = sums[:, other].astype(BF16)
     swap = to_mate(core_out, core_got, 0, mates[0])
     swap.start()
+    fold_turn(1)
     lax.fori_loop(0, 2, outer, 0)
-    start(fold, 0)
+    fold_start(0)
 
     Q = H // XS
     swap.wait()
@@ -322,7 +428,7 @@
         cp = to_mate(x_out.at[d - 1], x_got.at[d - 1], d, mates[1 + d])
         cp.start()
         spread.append(cp)
-    lax.fori_loop(0, 2, inner, 0)
+    fold_turn(0)
     acc = sums[:, pl.ds(pl.multiple_of(core * H + xi * Q, Q), Q)]
     for d in range(1, XS):
         spread[d - 1].wait()
@@ -330,6 +436,7 @@
     z_out[...] = acc.astype(BF16)
     cross = to_mate(z_out, z_got, XS, mates[1])
     cross.start()
+    lax.fori_loop(0, 2, inner, 0)
     for k in range(8):
         add_fold(1, k)
     cross.wait()
@@ -353,8 +460,15 @@
     for k in range(4):
         grad[k] = center[k].astype(BF16)
     for s in range(2):
-        sent(halo, s)
-        sent(fold, s)
+        halo_sent(s)
+        fold_sent(s)
+
+
+def widen_kernel(grad, probe, wide_grad, wide_probe):
+    for k in range(4):
+        wide_grad[k] = grad[k].astype(F32)
+    for k in range(2):
+        wide_probe[k] = probe[k].astype(F32)
 
 
 def tables():
@@ -385,11 +499,17 @@
             pltpu.VMEM((3, H, W), BF16), pltpu.VMEM((3, H, W), BF16),
             pltpu.VMEM((XS - 1, 3, Q, W), BF16), pltpu.VMEM((XS - 1, 3, Q, W), BF16),
             pltpu.VMEM((3, Q, W), BF16), pltpu.VMEM((3, Q, W), BF16), pltpu.VMEM((4, W, W), F32),
-            dma((2,)), dma((2, 8)), dma((2, 8)), dma((2, 8)), dma((2, 8)), dma((2 * XS + 1,)), dma((2 * XS + 1,)),
+            pltpu.VMEM((2, 4, 2, H, H), BF16), dma((2,)), dma((2, 4)), dma((2, 4)), dma((2, 8)), dma((2, 8)), dma((2, 8)), dma((2, 8)), dma((2 * XS + 1,)), dma((2 * XS + 1,)),
         ],
         compiler_params=pltpu.CompilerParams(collective_id=0, has_side_effects=True, vmem_limit_bytes=60 << 20),
     )(positions.T, object_slices.reshape(4, W, W), probe_wave_parts[0], prop_phase, measured, tables())
-    return grad.reshape(2, 2, W, W).astype(F32), probe_grad[None].astype(F32)
+    wide_grad, wide_probe = pl.pallas_call(
+        widen_kernel,
+        out_shape=(shape((4, W, W), F32), shape((2, W, W), F32)),
+        in_specs=[vm, vm],
+        out_specs=(vm, vm),
+    )(grad, probe_grad)
+    return wide_grad.reshape(2, 2, W, W), wide_probe[None]
 
 
 def solution(mesh):

time: 68.7 us -> 65.1 us (0.948)
  the two profiles are of different devices: /device:TPU:129 before, /device:TPU:133 now
where the time goes in v3:
time: 65.1 us; the launch traced here: 65 us
  Pallas kernels  64.3 us (99%)
    pallas_call x1, Pallas kernels, on_device(): pl.pallas_call(functools.partial(kernel, n_row, n_col), out_shape=(shape(...  62 us
    pallas_call x1, Pallas kernels, on_device(): pl.pallas_call(widen_kernel, out_shape=(shape((4, W, W), F32), shape((2,...  2.32 us

profile of v3, /device:TPU:133, one launch (start us, length us, event | category | flops | bytes accessed | tf_op | source)
XLA Modules:
  0.0 65.0 jit_solution(2685875723841971092)
XLA Ops:
  0.6 62.0 %shard_map.77 = (bf16[4,256,256]{2,1,0:T(8,128)(2,1)}, bf16[2,256,256]{2,1,0:T(8,128)(2,1)}) custom-call(s32[2,4]{1,0:T(2,128)} %bitcast.7, bf16[4,256,256]{2,1,0:T(8,128)(2,1)} %bitcast.5, f32[2,256,256]{2,1,0:T(8,128)} %bitcast.6, f32[256,256]{1,0:T(8,128)} %phase.1, f32[4,256,256]{2,1,0:T(8,128)} %meas_in.1, bf16[2,256,256]{2,1,0:T(8,128)(2,1)} %constant.6.cs), custom_call_target="tpu_custom_call" | custom-call | tf_op jit(solution)/shard_map/pallas_call | solution.py:487
  62.7 2.3 %shard_map.78 = (f32[4,256,256]{2,1,0:T(8,128)}, f32[2,256,256]{2,1,0:T(8,128)}) custom-call(bf16[4,256,256]{2,1,0:T(8,128)(2,1)} %get-tuple-element.6.grad, bf16[2,256,256]{2,1,0:T(8,128)(2,1)} %get-tuple-element.7.probe), custom_call_target="tpu_custom_call" | custom-call | tf_op jit(solution)/shard_map/pallas_call | solution.py:506

commit v4 on v3

--- a/solution.py
+++ b/solution.py
@@ -40,11 +40,11 @@
 
 def kernel(
     n_row, n_col,
-    pos, obj, probe, phase, meas_in, cs,
-    grad, fin,
-    fwd_t, inv_t, prop, u, v, h, ext, pr, wave, g, sums, meas,
+    pos, obj, probe_in, phase_in, meas_in, cs_in,
+    center, fin,
+    probe, phase, cs, fwd_t, inv_t, prop, u, v, h, ext, pr, wave, g, sums, meas,
     out_row, out_col, got_row, got_col,
-    core_out, core_got, x_out, x_got, z_out, z_got, center,
+    core_out, core_got, x_out, x_got, z_out, z_got,
     turned, local_sem, turn_send, turn_recv, halo_send, halo_recv, fold_send, fold_recv, sum_send, sum_recv,
 ):
     r, c = lax.axis_index("row"), lax.axis_index("col")
@@ -85,18 +85,26 @@
     mates = [(row_at(zi, xi, 1 - core), c), (row_at(1 - zi, xi, core), c)]
     mates += [(row_at(zi, lax.rem(xi + d, XS), core), c) for d in range(1, XS)]
 
+    crossed = [(row_at(zi, lax.rem(xi + d, XS), 1 - core), c) for d in range(1, XS)]
+
     barrier = pltpu.get_barrier_semaphore()
     for dr, dc in AROUND:
         @pl.when(inside(dr, dc))
         def _():
             pl.semaphore_signal(barrier, inc=1, device_id=(r + dr, c + dc), device_id_type=MESH)
-    for mate in mates[1:]:
+    for mate in mates[1:] + crossed:
         pl.semaphore_signal(barrier, inc=1, device_id=mate, device_id_type=MESH)
     own = pltpu.make_async_copy(obj, ext.at[:, pl.ds(H, W), pl.ds(H, W)], local_sem.at[0])
     own.start()
     load = pltpu.make_async_copy(meas_in, meas, local_sem.at[1])
     load.start()
-    peers = jnp.int32(len(mates) - 1)
+    small = [
+        pltpu.make_async_copy(a, b, local_sem.at[2 + i])
+        for i, (a, b) in enumerate(((probe_in, probe), (phase_in, phase), (cs_in, cs)))
+    ]
+    for cp in small:
+        cp.start()
+    peers = jnp.int32(len(mates) - 1 + len(crossed))
     for dr, dc in AROUND:
         peers = peers + inside(dr, dc).astype(jnp.int32)
     pl.semaphore_wait(barrier, peers)
@@ -242,6 +250,8 @@
             e, f = rim_of(dr), rim_of(dc)
             ext[:, e, f] = jnp.zeros((4, e.stop - e.start, f.stop - f.start), BF16)
 
+    for cp in small:
+        cp.wait()
     cos_t, sin_t = cs[0], cs[1]
     for t, sgn in ((fwd_t, 1), (inv_t, -1)):
         t[0:W, 0:W] = cos_t
@@ -428,7 +438,7 @@
         cp = to_mate(x_out.at[d - 1], x_got.at[d - 1], d, mates[1 + d])
         cp.start()
         spread.append(cp)
-    fold_turn(0)
+    lax.fori_loop(0, 2, inner, 0)
     acc = sums[:, pl.ds(pl.multiple_of(core * H + xi * Q, Q), Q)]
     for d in range(1, XS):
         spread[d - 1].wait()
@@ -436,7 +446,7 @@
     z_out[...] = acc.astype(BF16)
     cross = to_mate(z_out, z_got, XS, mates[1])
     cross.start()
-    lax.fori_loop(0, 2, inner, 0)
+    fold_turn(0)
     for k in range(8):
         add_fold(1, k)
     cross.wait()
@@ -446,29 +456,25 @@
     fin[0, here] = (tot[0] * scale).astype(BF16)
     fin[1, here] = (tot[1] * scale).astype(BF16)
     gather = []
-    for d in range(1, XS):
-        cp = to_mate(fin.at[:, here], fin.at[:, here], XS + d, mates[1 + d])
+    for i, mate in enumerate(mates[2:] + crossed + mates[:1]):
+        cp = to_mate(fin.at[:, here], fin.at[:, here], XS + 1 + i, mate)
         cp.start()
         gather.append(cp)
-    for d in range(1, XS):
-        gather[d - 1].wait()
-    last = to_mate(fin.at[:, mine], fin.at[:, mine], 2 * XS, mates[0])
-    last.start()
     for k in (6, 7, 0, 1, 2, 3, 4, 5):
         add_fold(0, k)
-    last.wait()
-    for k in range(4):
-        grad[k] = center[k].astype(BF16)
+    for cp in gather:
+        cp.wait()
     for s in range(2):
         halo_sent(s)
         fold_sent(s)
 
 
-def widen_kernel(grad, probe, wide_grad, wide_probe):
-    for k in range(4):
-        wide_grad[k] = grad[k].astype(F32)
+def finish_kernel(grad, probe, grad_out, probe_out, sem):
+    put = pltpu.make_async_copy(grad, grad_out, sem)
+    put.start()
     for k in range(2):
-        wide_probe[k] = probe[k].astype(F32)
+        probe_out[k] = probe[k].astype(F32)
+    put.wait()
 
 
 def tables():
@@ -486,10 +492,11 @@
     dma = pltpu.SemaphoreType.DMA
     grad, probe_grad = pl.pallas_call(
         functools.partial(kernel, n_row, n_col),
-        out_shape=(shape((4, W, W), BF16), shape((2, W, W), BF16)),
-        in_specs=[pl.BlockSpec(memory_space=pltpu.SMEM), anys, vm, vm, anys, vm],
+        out_shape=(pltpu.VMEM((4, W, W), F32), pltpu.VMEM((2, W, W), BF16)),
+        in_specs=[pl.BlockSpec(memory_space=pltpu.SMEM)] + [anys] * 5,
         out_specs=(vm, vm),
         scratch_shapes=[
+            pltpu.VMEM((2, W, W), F32), pltpu.VMEM((W, W), F32), pltpu.VMEM((2, W, W), BF16),
             pltpu.VMEM((2 * W, 2 * W), BF16), pltpu.VMEM((2 * W, 2 * W), BF16), pltpu.VMEM((2, W, W), F32),
             pltpu.VMEM((NP, 2 * W, W), BF16), pltpu.VMEM((NP, 2 * W, W), BF16), pltpu.VMEM((NP, W, 2 * W), BF16),
             pltpu.VMEM((4, 2 * W, 2 * W), BF16), pltpu.VMEM((NP, 2, W, W), F32), pltpu.VMEM((NP, 2, W, W), F32),
@@ -498,18 +505,19 @@
             pltpu.VMEM((2, 4, H, 2 * W), BF16), pltpu.VMEM((2, 4, W, H), BF16),
             pltpu.VMEM((3, H, W), BF16), pltpu.VMEM((3, H, W), BF16),
             pltpu.VMEM((XS - 1, 3, Q, W), BF16), pltpu.VMEM((XS - 1, 3, Q, W), BF16),
-            pltpu.VMEM((3, Q, W), BF16), pltpu.VMEM((3, Q, W), BF16), pltpu.VMEM((4, W, W), F32),
-            pltpu.VMEM((2, 4, 2, H, H), BF16), dma((2,)), dma((2, 4)), dma((2, 4)), dma((2, 8)), dma((2, 8)), dma((2, 8)), dma((2, 8)), dma((2 * XS + 1,)), dma((2 * XS + 1,)),
+            pltpu.VMEM((3, Q, W), BF16), pltpu.VMEM((3, Q, W), BF16),
+            pltpu.VMEM((2, 4, 2, H, H), BF16), dma((5,)), dma((2, 4)), dma((2, 4)), dma((2, 8)), dma((2, 8)), dma((2, 8)), dma((2, 8)), dma((3 * XS,)), dma((3 * XS,)),
         ],
         compiler_params=pltpu.CompilerParams(collective_id=0, has_side_effects=True, vmem_limit_bytes=60 << 20),
     )(positions.T, object_slices.reshape(4, W, W), probe_wave_parts[0], prop_phase, measured, tables())
-    wide_grad, wide_probe = pl.pallas_call(
-        widen_kernel,
+    grad_out, probe_out = pl.pallas_call(
+        finish_kernel,
         out_shape=(shape((4, W, W), F32), shape((2, W, W), F32)),
         in_specs=[vm, vm],
-        out_specs=(vm, vm),
-    )(grad, probe_grad)
-    return wide_grad.reshape(2, 2, W, W), wide_probe[None]
+        out_specs=(anys, vm),
+        scratch_shapes=[dma],
+    )(pltpu.with_memory_space_constraint(grad, pltpu.VMEM), pltpu.with_memory_space_constraint(probe_grad, pltpu.VMEM))
+    return grad_out.reshape(2, 2, W, W), probe_out[None]
 
 
 def solution(mesh):

time: 65.1 us -> 62.7 us (0.963)
  the two profiles are of different devices: /device:TPU:133 before, /device:TPU:129 now
where the time goes in v4:
time: 62.7 us; the launch traced here: 62.5 us
  Pallas kernels  61.7 us (98%)
  between operations  0.8 us (1%)
    pallas_call x1, Pallas kernels, on_device(): pl.pallas_call(functools.partial(kernel, n_row, n_col), out_shape=(pltpu....  60 us
    pallas_call x1, Pallas kernels, on_device(): pl.pallas_call(finish_kernel, out_shape=(shape((4, W, W), F32), shape((2,...  1.77 us

profile of v4, /device:TPU:129, one launch (start us, length us, event | category | flops | bytes accessed | tf_op | source)
XLA Modules:
  0.0 62.5 jit_solution(3634195330457724190)
XLA Ops:
  0.6 60.0 %shard_map.77 = (f32[4,256,256]{2,1,0:T(8,128)S(1)}, bf16[2,256,256]{2,1,0:T(8,128)(2,1)S(1)}) custom-call(s32[2,4]{1,0:T(2,128)} %bitcast.7, bf16[4,256,256]{2,1,0:T(8,128)(2,1)} %bitcast.5, f32[2,256,256]{2,1,0:T(8,128)} %bitcast.6, f32[256,256]{1,0:T(8,128)} %phase_in.1, f32[4,256,256]{2,1,0:T(8,128)} %meas_in.1, bf16[2,256,256]{2,1,0:T(8,128)(2,1)} %constant.6.cs_in), custom_call_target="tpu_custom_call" | custom-call | tf_op jit(solution)/shard_map/pallas_call | solution.py:493
  60.6 1.8 %shard_map.78 = (f32[4,256,256]{2,1,0:T(8,128)}, f32[2,256,256]{2,1,0:T(8,128)}) custom-call(f32[4,256,256]{2,1,0:T(8,128)S(1)} %get-tuple-element.6.grad, bf16[2,256,256]{2,1,0:T(8,128)(2,1)S(1)} %get-tuple-element.7.probe), custom_call_target="tpu_custom_call" | custom-call | tf_op jit(solution)/shard_map/pallas_call | solution.py:513

commit v5 on v4

--- a/solution.py
+++ b/solution.py
@@ -17,6 +17,7 @@
 MESH = pl.DeviceIdType.MESH
 AROUND = ((-1, 0), (1, 0), (-1, -1), (-1, 1), (1, -1), (1, 1), (0, -1), (0, 1))
 CHUNKS = [slice(i, i + RC) for i in range(0, W, RC)]
+PARTS = [slice(0, H), slice(H, W)]
 XS, ZS = 4, 2
 LOOP = 8
 TURNS = [(dr, dc) for dc in (-1, 1) for dr in (-1, 1)]
@@ -326,7 +327,12 @@
     def e2(n, q, re, im):
         wave[n, 0, q] = re
         wave[n, 1, q] = im
-    sweep(first_exit, bright, transform(u, fwd_t, inv_t, e1))
+    into_spectrum = transform(u, fwd_t, inv_t, e1)
+
+    def spectrum(n):
+        into_spectrum(n)
+        bright(n)
+    sweep(first_exit, spectrum)
     halo_turn(1)
     sweep(transform(u, inv_t, fwd_t, e2))
 
@@ -352,34 +358,34 @@
         v[n, moved(q, W)] = (a * im - b * re).astype(BF16)
     sweep(second_exit, transform(u, fwd_t, inv_t, e3), transform(u, inv_t, fwd_t, e4))
 
-    def total(plane, q, a, b, cols):
-        acc = None
-        for n in range(NP):
-            row = lax.broadcasted_iota(jnp.int32, (q.stop - q.start, H), 0) + q.start
-            col = lax.broadcasted_iota(jnp.int32, (q.stop - q.start, H), 1) + cols.start
-            m = (row >= pos[0, n]) if a == 0 else (row < pos[0, n])
-            m = m & ((col >= pos[1, n]) if b == 0 else (col < pos[1, n]))
-            part = jnp.where(m, g[n, plane, q, cols], 0.0)
-            acc = part if acc is None else acc + part
-        return acc
-
-    lo, hi = slice(0, H), slice(H, W)
-
-    def outer(plane, _):
-        for j in range(4):
-            out_row[0, plane, :, j * H:(j + 1) * H] = total(plane, lo, 0, j // 2, (lo, hi)[j % 2]).astype(BF16)
-            out_row[1, plane, :, j * H:(j + 1) * H] = total(plane, hi, 1, j // 2, (lo, hi)[j % 2]).astype(BF16)
-        for i, q in enumerate((hi, lo)):
-            rows = slice(i * H, (i + 1) * H)
-            out_col[0, plane, rows] = total(plane, q, i, 0, lo).astype(BF16)
-            out_col[1, plane, rows] = total(plane, q, i, 1, hi).astype(BF16)
-        return 0
-
-    def inner(plane, _):
-        for i, q in enumerate((hi, lo)):
-            rows = slice(i * H, (i + 1) * H)
-            center[plane, rows, 0:H] = total(plane, q, i, 0, hi)
-            center[plane, rows, H:] = total(plane, q, i, 1, lo)
+    def place(plane, _):
+        for p, q in enumerate(PARTS):
+            for o, f in enumerate(PARTS):
+                row = lax.broadcasted_iota(jnp.int32, (H, H), 0) + q.start
+                col = lax.broadcasted_iota(jnp.int32, (H, H), 1) + f.start
+                every = upper = fore = both = None
+                for n in range(NP):
+                    x = g[n, plane, q, f]
+                    x_up = jnp.where(row >= pos[0, n], x, 0.0)
+                    x_fore = jnp.where(col >= pos[1, n], x, 0.0)
+                    x_both = jnp.where(col >= pos[1, n], x_up, 0.0)
+                    if n == 0:
+                        every, upper, fore, both = x, x_up, x_fore, x_both
+                    else:
+                        every, upper, fore, both = every + x, upper + x_up, fore + x_fore, both + x_both
+                back_up = upper - both
+                down_fore = fore - both
+                parts = {(0, 0): both, (0, 1): back_up, (1, 0): down_fore, (1, 1): every - fore - back_up}
+                for (a, b), val in parts.items():
+                    j = 2 * b + o
+                    if a == p:
+                        out_row[a, plane, :, j * H:(j + 1) * H] = val.astype(BF16)
+                    else:
+                        rows = slice(a * H, (a + 1) * H)
+                        if b == o:
+                            out_col[b, plane, rows] = val.astype(BF16)
+                        else:
+                            center[plane, rows, b * H:(b + 1) * H] = val
         return 0
 
     def add_fold(s, k):
@@ -397,10 +403,9 @@
                     got = got_col[0 if dc < 0 else 1, plane]
                 center[plane, e, f] += got.astype(F32)
 
-    lax.fori_loop(2, 4, outer, 0)
+    lax.fori_loop(2, 4, place, 0)
     fold_start(1)
 
-    lax.fori_loop(2, 4, inner, 0)
 
     def e5(n, q, re, im):
         p, t = prop[0, q], prop[1, q]
@@ -417,7 +422,12 @@
     def probe_back(n):
         sums[0] += back(wave[n, 0], n)
         sums[1] += back(wave[n, 1], n)
-    sweep(transform(v, fwd_t, inv_t, e5), transform(u, inv_t, fwd_t, e6), probe_back)
+    last = transform(u, inv_t, fwd_t, e6)
+
+    def last_and_back(n):
+        last(n)
+        probe_back(n)
+    sweep(transform(v, fwd_t, inv_t, e5), last_and_back)
 
     mine = pl.ds(pl.multiple_of(core * H, H), H)
     other = pl.ds(pl.multiple_of((1 - core) * H, H), H)
@@ -425,7 +435,7 @@
     swap = to_mate(core_out, core_got, 0, mates[0])
     swap.start()
     fold_turn(1)
-    lax.fori_loop(0, 2, outer, 0)
+    lax.fori_loop(0, 2, place, 0)
     fold_start(0)
 
     Q = H // XS
@@ -438,7 +448,6 @@
         cp = to_mate(x_out.at[d - 1], x_got.at[d - 1], d, mates[1 + d])
         cp.start()
         spread.append(cp)
-    lax.fori_loop(0, 2, inner, 0)
     acc = sums[:, pl.ds(pl.multiple_of(core * H + xi * Q, Q), Q)]
     for d in range(1, XS):
         spread[d - 1].wait()

time: 62.7 us -> 61.7 us (0.984)
  Pallas kernels: 61.7 us -> 60.7 us
    pallas_call x1, Pallas kernels: 60 us -> 59 us  [on_device(): pl.pallas_call(functools.partial(kernel, n_row, n_col), out_shape=(pltpu....]
where the time goes in v5:
time: 61.7 us; the launch traced here: 61.5 us
  Pallas kernels  60.7 us (98%)
  between operations  0.8 us (1%)
    pallas_call x1, Pallas kernels, on_device(): pl.pallas_call(functools.partial(kernel, n_row, n_col), out_shape=(pltpu....  59 us
    pallas_call x1, Pallas kernels, on_device(): pl.pallas_call(finish_kernel, out_shape=(shape((4, W, W), F32), shape((2,...  1.77 us

profile of v5, /device:TPU:129, one launch (start us, length us, event | category | flops | bytes accessed | tf_op | source)
XLA Modules:
  0.0 61.5 jit_solution(15244386621502856246)
XLA Ops:
  0.6 59.0 %shard_map.77 = (f32[4,256,256]{2,1,0:T(8,128)S(1)}, bf16[2,256,256]{2,1,0:T(8,128)(2,1)S(1)}) custom-call(s32[2,4]{1,0:T(2,128)} %bitcast.7, bf16[4,256,256]{2,1,0:T(8,128)(2,1)} %bitcast.5, f32[2,256,256]{2,1,0:T(8,128)} %bitcast.6, f32[256,256]{1,0:T(8,128)} %phase_in.1, f32[4,256,256]{2,1,0:T(8,128)} %meas_in.1, bf16[2,256,256]{2,1,0:T(8,128)(2,1)} %constant.6.cs_in), custom_call_target="tpu_custom_call" | custom-call | tf_op jit(solution)/shard_map/pallas_call | solution.py:502
  59.6 1.8 %shard_map.78 = (f32[4,256,256]{2,1,0:T(8,128)}, f32[2,256,256]{2,1,0:T(8,128)}) custom-call(f32[4,256,256]{2,1,0:T(8,128)S(1)} %get-tuple-element.6.grad, bf16[2,256,256]{2,1,0:T(8,128)(2,1)S(1)} %get-tuple-element.7.probe), custom_call_target="tpu_custom_call" | custom-call | tf_op jit(solution)/shard_map/pallas_call | solution.py:522

commit v6 on v5

--- a/solution.py
+++ b/solution.py
@@ -307,6 +307,41 @@
         return pltpu.roll(pltpu.roll(x, W - pos[0, n], 0), W - pos[1, n], 1)
 
     halo_turn(0)
+    Q = H // XS
+    mine = pl.ds(pl.multiple_of(core * H, H), H)
+    other = pl.ds(pl.multiple_of((1 - core) * H, H), H)
+    GROUPS = (slice(0, 2), slice(2, 3))
+
+    def swap_start(i):
+        p = GROUPS[i]
+        core_out[p] = sums[p, other].astype(BF16)
+        cp = to_mate(core_out.at[p], core_got.at[p], i * (XS + 1), mates[0])
+        cp.start()
+        return cp
+
+    def spread_start(i, cp):
+        p = GROUPS[i]
+        cp.wait()
+        sums[p, mine] = sums[p, mine] + core_got[p].astype(F32)
+        cps = []
+        for d in range(1, XS):
+            at = pl.multiple_of(core * H + lax.rem(xi + d, XS) * Q, Q)
+            x_out[d - 1, p] = sums[p, pl.ds(at, Q)].astype(BF16)
+            cps.append(to_mate(x_out.at[d - 1, p], x_got.at[d - 1, p], i * (XS + 1) + d, mates[1 + d]))
+            cps[-1].start()
+        return cps
+
+    def cross_start(i, cps):
+        p = GROUPS[i]
+        acc = sums[p, pl.ds(pl.multiple_of(core * H + xi * Q, Q), Q)]
+        for d in range(1, XS):
+            cps[d - 1].wait()
+            acc = acc + x_got[d - 1, p].astype(F32)
+        z_out[p] = acc.astype(BF16)
+        cp = to_mate(z_out.at[p], z_got.at[p], i * (XS + 1) + XS, mates[1])
+        cp.start()
+        return cp
+
     own.wait()
     halo_arrived(0)
 
@@ -333,6 +368,7 @@
         into_spectrum(n)
         bright(n)
     sweep(first_exit, spectrum)
+    swap_light = swap_start(1)
     halo_turn(1)
     sweep(transform(u, inv_t, fwd_t, e2))
 
@@ -405,6 +441,7 @@
 
     lax.fori_loop(2, 4, place, 0)
     fold_start(1)
+    light = spread_start(1, swap_light)
 
 
     def e5(n, q, re, im):
@@ -427,38 +464,21 @@
     def last_and_back(n):
         last(n)
         probe_back(n)
-    sweep(transform(v, fwd_t, inv_t, e5), last_and_back)
-
-    mine = pl.ds(pl.multiple_of(core * H, H), H)
-    other = pl.ds(pl.multiple_of((1 - core) * H, H), H)
-    core_out[...] = sums[:, other].astype(BF16)
-    swap = to_mate(core_out, core_got, 0, mates[0])
-    swap.start()
+    sweep(transform(v, fwd_t, inv_t, e5))
     fold_turn(1)
+    sweep(last_and_back)
+
+    swap = swap_start(0)
+    cross_light = cross_start(1, light)
     lax.fori_loop(0, 2, place, 0)
     fold_start(0)
-
-    Q = H // XS
-    swap.wait()
-    sums[:, mine] = sums[:, mine] + core_got[...].astype(F32)
-    spread = []
-    for d in range(1, XS):
-        at = pl.multiple_of(core * H + lax.rem(xi + d, XS) * Q, Q)
-        x_out[d - 1] = sums[:, pl.ds(at, Q)].astype(BF16)
-        cp = to_mate(x_out.at[d - 1], x_got.at[d - 1], d, mates[1 + d])
-        cp.start()
-        spread.append(cp)
-    acc = sums[:, pl.ds(pl.multiple_of(core * H + xi * Q, Q), Q)]
-    for d in range(1, XS):
-        spread[d - 1].wait()
-        acc = acc + x_got[d - 1].astype(F32)
-    z_out[...] = acc.astype(BF16)
-    cross = to_mate(z_out, z_got, XS, mates[1])
-    cross.start()
+    spread = spread_start(0, swap)
+    cross = cross_start(0, spread)
     fold_turn(0)
     for k in range(8):
         add_fold(1, k)
     cross.wait()
+    cross_light.wait()
     tot = z_out[...].astype(F32) + z_got[...].astype(F32)
     scale = 1.0 / jnp.sqrt(tot[2] + 1e-06)
     here = pl.ds(pl.multiple_of(core * H + xi * Q, Q), Q)
@@ -466,7 +486,7 @@
     fin[1, here] = (tot[1] * scale).astype(BF16)
     gather = []
     for i, mate in enumerate(mates[2:] + crossed + mates[:1]):
-        cp = to_mate(fin.at[:, here], fin.at[:, here], XS + 1 + i, mate)
+        cp = to_mate(fin.at[:, here], fin.at[:, here], 2 * (XS + 1) + i, mate)
         cp.start()
         gather.append(cp)
     for k in (6, 7, 0, 1, 2, 3, 4, 5):
@@ -479,11 +499,13 @@
 
 
 def finish_kernel(grad, probe, grad_out, probe_out, sem):
-    put = pltpu.make_async_copy(grad, grad_out, sem)
-    put.start()
+    puts = [pltpu.make_async_copy(grad.at[k], grad_out.at[k], sem.at[k]) for k in range(4)]
+    for put in puts:
+        put.start()
     for k in range(2):
         probe_out[k] = probe[k].astype(F32)
-    put.wait()
+    for put in puts:
+        put.wait()
 
 
 def tables():
@@ -515,7 +537,7 @@
             pltpu.VMEM((3, H, W), BF16), pltpu.VMEM((3, H, W), BF16),
             pltpu.VMEM((XS - 1, 3, Q, W), BF16), pltpu.VMEM((XS - 1, 3, Q, W), BF16),
             pltpu.VMEM((3, Q, W), BF16), pltpu.VMEM((3, Q, W), BF16),
-            pltpu.VMEM((2, 4, 2, H, H), BF16), dma((5,)), dma((2, 4)), dma((2, 4)), dma((2, 8)), dma((2, 8)), dma((2, 8)), dma((2, 8)), dma((3 * XS,)), dma((3 * XS,)),
+            pltpu.VMEM((2, 4, 2, H, H), BF16), dma((5,)), dma((2, 4)), dma((2, 4)), dma((2, 8)), dma((2, 8)), dma((2, 8)), dma((2, 8)), dma((4 * XS + 1,)), dma((4 * XS + 1,)),
         ],
         compiler_params=pltpu.CompilerParams(collective_id=0, has_side_effects=True, vmem_limit_bytes=60 << 20),
     )(positions.T, object_slices.reshape(4, W, W), probe_wave_parts[0], prop_phase, measured, tables())
@@ -524,7 +546,7 @@
         out_shape=(shape((4, W, W), F32), shape((2, W, W), F32)),
         in_specs=[vm, vm],
         out_specs=(anys, vm),
-        scratch_shapes=[dma],
+        scratch_shapes=[dma((4,))],
     )(pltpu.with_memory_space_constraint(grad, pltpu.VMEM), pltpu.with_memory_space_constraint(probe_grad, pltpu.VMEM))
     return grad_out.reshape(2, 2, W, W), probe_out[None]
 

time: 61.7 us -> 65.2 us (1.057)
  the two profiles are of different devices: /device:TPU:129 before, /device:TPU:133 now
where the time goes in v6:
time: 65.2 us; the launch traced here: 65 us
  Pallas kernels  64.2 us (98%)
  between operations  0.8 us (1%)
    pallas_call x1, Pallas kernels, on_device(): pl.pallas_call(functools.partial(kernel, n_row, n_col), out_shape=(pltpu....  62.4 us
    pallas_call x1, Pallas kernels, on_device(): pl.pallas_call(finish_kernel, out_shape=(shape((4, W, W), F32), shape((2,...  1.79 us

profile of v6, /device:TPU:133, one launch (start us, length us, event | category | flops | bytes accessed | tf_op | source)
XLA Modules:
  0.0 65.0 jit_solution(16077819807643657427)
XLA Ops:
  0.6 62.4 %shard_map.77 = (f32[4,256,256]{2,1,0:T(8,128)S(1)}, bf16[2,256,256]{2,1,0:T(8,128)(2,1)S(1)}) custom-call(s32[2,4]{1,0:T(2,128)} %bitcast.7, bf16[4,256,256]{2,1,0:T(8,128)(2,1)} %bitcast.5, f32[2,256,256]{2,1,0:T(8,128)} %bitcast.6, f32[256,256]{1,0:T(8,128)} %phase_in.1, f32[4,256,256]{2,1,0:T(8,128)} %meas_in.1, bf16[2,256,256]{2,1,0:T(8,128)(2,1)} %constant.6.cs_in), custom_call_target="tpu_custom_call" | custom-call | tf_op jit(solution)/shard_map/pallas_call | solution.py:524
  63.1 1.8 %shard_map.78 = (f32[4,256,256]{2,1,0:T(8,128)}, f32[2,256,256]{2,1,0:T(8,128)}) custom-call(f32[4,256,256]{2,1,0:T(8,128)S(1)} %get-tuple-element.6.grad, bf16[2,256,256]{2,1,0:T(8,128)(2,1)S(1)} %get-tuple-element.7.probe), custom_call_target="tpu_custom_call" | custom-call | tf_op jit(solution)/shard_map/pallas_call | solution.py:544

commit v7 on v5

--- a/solution.py
+++ b/solution.py
@@ -434,9 +434,9 @@
     core_out[...] = sums[:, other].astype(BF16)
     swap = to_mate(core_out, core_got, 0, mates[0])
     swap.start()
-    fold_turn(1)
     lax.fori_loop(0, 2, place, 0)
     fold_start(0)
+    fold_turn(1)
 
     Q = H // XS
     swap.wait()

time: 61.7 us -> 61.4 us (level)
  no operation moved by 1% of the time
where the time goes in v7:
time: 61.4 us; the launch traced here: 61.3 us
  Pallas kernels  60.5 us (99%)
  between operations  0.8 us (1%)
    pallas_call x1, Pallas kernels, on_device(): pl.pallas_call(functools.partial(kernel, n_row, n_col), out_shape=(pltpu....  58.7 us
    pallas_call x1, Pallas kernels, on_device(): pl.pallas_call(finish_kernel, out_shape=(shape((4, W, W), F32), shape((2,...  1.77 us

profile of v7, /device:TPU:129, one launch (start us, length us, event | category | flops | bytes accessed | tf_op | source)
XLA Modules:
  0.0 61.3 jit_solution(992905636170981546)
XLA Ops:
  0.6 58.7 %shard_map.77 = (f32[4,256,256]{2,1,0:T(8,128)S(1)}, bf16[2,256,256]{2,1,0:T(8,128)(2,1)S(1)}) custom-call(s32[2,4]{1,0:T(2,128)} %bitcast.7, bf16[4,256,256]{2,1,0:T(8,128)(2,1)} %bitcast.5, f32[2,256,256]{2,1,0:T(8,128)} %bitcast.6, f32[256,256]{1,0:T(8,128)} %phase_in.1, f32[4,256,256]{2,1,0:T(8,128)} %meas_in.1, bf16[2,256,256]{2,1,0:T(8,128)(2,1)} %constant.6.cs_in), custom_call_target="tpu_custom_call" | custom-call | tf_op jit(solution)/shard_map/pallas_call | solution.py:502
  59.4 1.8 %shard_map.78 = (f32[4,256,256]{2,1,0:T(8,128)}, f32[2,256,256]{2,1,0:T(8,128)}) custom-call(f32[4,256,256]{2,1,0:T(8,128)S(1)} %get-tuple-element.6.grad, bf16[2,256,256]{2,1,0:T(8,128)(2,1)S(1)} %get-tuple-element.7.probe), custom_call_target="tpu_custom_call" | custom-call | tf_op jit(solution)/shard_map/pallas_call | solution.py:522
